TPU v7x, 32 devices: a whole 2x2x4 slice. The times are simulated.
32 devices in a mesh: slab: 8 (over z, x), tile: 4 (over y, core).
Axes of the slice: x: 2, y: 2, z: 4, core: 2. Of those that a mesh axis runs over, the one named last changes fastest.
Arguments:
- fixed_planes: float32 [128, 512, 128], P(('slab', 'tile')), may hold values from -6 to 6
- moving_planes: float32 [2, 128, 512, 128], P(None, ('slab', 'tile')), may hold values from -6 to 6
- pair_dest: int32 [2, 128], P(None, ('slab', 'tile')), may hold values from 0 to 7, as said below
- pair_slot: int32 [2, 128], P(None, ('slab', 'tile')), may hold values from 0 to 3, as said below
- plane_shift: int32 [2, 2, 128], P(None, None, ('slab', 'tile')), may hold values from -24 to 24
- live_count: int32 [32], P(('slab', 'tile')), may hold values from 1 to 4, 74 in all
- piece_block: int32 [2048], P(('slab', 'tile')), may hold values from 0 to 511, as said below
Outputs:
- peaks: float32 [2, 128], P(None, ('slab', 'tile'))
- blocks: float32 [512, 32, 128], P(('slab', 'tile'))
Inputs may be any that keep to these rules, and one draw needn't show every extreme that they name: `pair_dest`: round 0 entries lie in 0 to 7 and round 1 entries in 0 to 3. With pair_slot, every fixed plane of every device is targeted by exactly one moving plane in each round. In round 0 no device targets more than 2 planes of any one device, in round 1 no more than 2; in every round every device targets exactly that many planes of some device. `pair_slot`: drawn together with pair_dest. `live_count`: the counts sum to 74 and some device has 4. `piece_block`: block b is owned by device b // 16 along slab+tile. At most 2 pieces of one device go to blocks of one owner, and the first 2 pieces of every device go to blocks of one owner.
All inputs are finite; a program needn't handle non-finite values.
Results may differ from a plain program's by a relative error of at most 0.0003.
Values sent between devices are 32-bit elements; how exact they have to be, the bound alone decides.
No kernel may reach another device: no remote copies, remote signals or barrier semaphores. Data moves between devices by JAX's collectives and lax.ppermute only.
A program may use at most 128 MiB of HBM per device.

v0:
```python
import functools
import math

import jax
import jax.numpy as jnp
import numpy as np
from jax import lax
from jax.experimental import pallas as pl
from jax.experimental.pallas import tpu as pltpu
from jax.sharding import PartitionSpec as P

PIECES = 16
OWNED = 16
FLOOR = 0.25
CENTER = 4.0
PAD = 16
TILE = 8
F32, BF16, I32 = jnp.float32, jnp.bfloat16, jnp.int32
VMEM = pl.BlockSpec(memory_space=pltpu.VMEM)
HBM = pl.BlockSpec(memory_space=pltpu.HBM)
SMEM = pl.BlockSpec(memory_space=pltpu.SMEM)


def halves(table):
    high = np.asarray(table, np.float32).astype(jnp.bfloat16)
    low = np.asarray(table - high.astype(np.float64), np.float32).astype(jnp.bfloat16)
    return high, low


@functools.lru_cache
def tables(height, breadth):
    half, quarter = height // 2, height // 4
    rows = np.arange(half)
    even = np.arange(quarter)[:, None] * 2 * rows[None, :] % height * (2 * math.pi / height)
    odd = (np.arange(quarter)[:, None] * 2 + 1) * rows[None, :] % height * (2 * math.pi / height)
    scale = 1 / math.sqrt(height)
    alternating = np.cos(math.pi * rows)
    even_sine = -np.sin(even)
    even_sine[0] = alternating
    ahead_even = np.concatenate([np.cos(even), even_sine], 0) * scale
    ahead_odd = np.concatenate([np.cos(odd), -np.sin(odd)], 0) * scale
    back_cosine = 2 * np.cos(even)
    back_cosine[0] = 1
    back_sine = 2 * np.sin(even)
    back_sine[0] = alternating
    back_even = np.concatenate([back_cosine, back_sine], 0).T * scale
    back_odd = np.concatenate([2 * np.cos(odd), 2 * np.sin(odd)], 0).T * scale
    index = np.arange(breadth)
    angle = index[:, None] * index[None, :] % breadth * (2 * math.pi / breadth)
    cosine, sine = np.cos(angle) / math.sqrt(breadth), np.sin(angle) / math.sqrt(breadth)
    across = np.block([[cosine, -sine], [sine, cosine]])
    pairs = [halves(t) for t in (ahead_even, ahead_odd, across, back_even, back_odd)]
    return [half_table for pair in pairs for half_table in pair]


def split(x):
    high = x.astype(BF16)
    return high, (x - high.astype(F32)).astype(BF16)


def dot(a, b):
    return jnp.dot(a, b, preferred_element_type=F32)


def table_times(high, low, x):
    x_high, x_low = split(x)
    breadth = x.shape[1]
    both = dot(high[...], jnp.concatenate([x_high, x_low], 1))
    return both[:, :breadth] + both[:, breadth:] + dot(low[...], x_high)


def times_table(x, high, low):
    x_high, x_low = split(x)
    return dot(x_high, high[...]) + (dot(x_low, high[...]) + dot(x_high, low[...]))


def rows_of(shape):
    return lax.broadcasted_iota(I32, shape, 0)


def forward(x, even, odd, across):
    height, breadth = x.shape
    half, quarter = height // 2, height // 4
    top, bottom = x[:half], x[half:]
    e = table_times(*even, top + bottom)
    o = table_times(*odd, top - bottom)
    first = rows_of((quarter, breadth)) == 0
    sine = e[quarter:]
    last = jnp.where(rows_of((PAD, breadth)) == 0, sine[:PAD], 0.0)
    mixed = jnp.concatenate(
        [
            jnp.concatenate([e[:quarter], jnp.where(first, 0.0, sine)], 1),
            jnp.concatenate([o[:quarter], o[quarter:]], 1),
            jnp.concatenate([last, jnp.zeros_like(last)], 1),
        ],
        0,
    )
    return times_table(mixed, *across)


def peak_of(fixed, moving, across, even, odd):
    breadth = fixed.shape[1] // 2
    half = fixed.shape[0] - PAD
    quarter = half // 2
    fr, fi = fixed[:, :breadth], fixed[:, breadth:]
    gr, gi = moving[:, :breadth], moving[:, breadth:]
    real = fr * gr + fi * gi
    minus = fr * gi - fi * gr
    factor = lax.rsqrt(real * real + minus * minus + FLOOR**2)
    v = times_table(jnp.concatenate([real * factor, minus * factor], 1), *across)
    vr, vn = v[:, :breadth], v[:, breadth:]
    first = rows_of((quarter, breadth)) == 0
    last = jnp.broadcast_to(vr[half : half + 1], (quarter, breadth))
    e = table_times(*even, jnp.concatenate([vr[:quarter], jnp.where(first, last, vn[:quarter])], 0))
    o = table_times(*odd, jnp.concatenate([vr[quarter:half], vn[quarter:half]], 0))
    highest = e + jnp.abs(o)
    return jnp.max(jnp.max(highest, axis=0, keepdims=True), axis=1, keepdims=True)


def weight_of(peak):
    return 1.0 / (1.0 + jnp.exp(-(peak - CENTER)))


def rolled(x, down, across):
    height, breadth = x.shape
    x = pltpu.roll(x, jnp.where(across < 0, across + breadth, across), 1)
    return pltpu.roll(x, jnp.where(down < 0, down + height, down), 0)


def choose(value, low, high, act):
    if high - low == 1:
        act(low)
        return
    middle = (low + high) // 2

    @pl.when(value < middle)
    def _():
        choose(value, low, middle, act)

    @pl.when(value >= middle)
    def _():
        choose(value, middle, high, act)


def spread_kernel(count, sizes, pieces_ref, dest_ref, slot_ref, live_ref, moving_ref, *rest):
    slab, tile, capacity = sizes
    outs, slots_ref = rest[:slab], rest[slab]
    labels, sem = rest[slab + 1 :]
    planes, height, breadth = moving_ref.shape[1:]
    run = height // slab
    here = lax.axis_index("slab")
    copies = []
    for k in reversed(range(slab)):
        rows = pl.ds(pl.multiple_of((here ^ k) * run, run), run)
        for s in range(planes):
            copy = pltpu.make_async_copy(
                moving_ref.at[0, s, rows], outs[k].at[pl.ds(s * run, run)], sem.at[k, s]
            )
            copy.start()
            copies.append(copy)
    pieces = pieces_ref[...]
    size = count
    row = jnp.broadcast_to(pieces, (size, size))
    i, j = rows_of((size, size)), lax.broadcasted_iota(I32, (size, size), 1)
    column = jnp.broadcast_to(
        jnp.sum(jnp.where(i == j, row, 0).astype(F32), axis=1, keepdims=True), (size, size)
    ).astype(I32)
    same = (lax.shift_right_arithmetic(row, 4) == lax.shift_right_arithmetic(column, 4)) & (i < j)
    rank = jnp.sum(same.astype(F32), axis=0, keepdims=True).astype(I32)
    place = lax.shift_right_arithmetic(pieces, 4) * capacity + rank
    slots_ref[...] = jnp.broadcast_to(place, slots_ref.shape)
    lane = lax.broadcasted_iota(I32, (1, size), 1)
    kept = lane < jnp.minimum(live_ref[0] * PIECES, count)
    within = jnp.where(kept, (pieces & (OWNED - 1)) + 1, 0).astype(F32)
    block = tile * capacity
    target = jnp.zeros((block, breadth), F32)
    for s in range(planes):
        value = (dest_ref[0, s] * planes + slot_ref[0, s]).astype(F32)
        target = jnp.where(rows_of((block, breadth)) == s, value, target)
    right = lax.broadcasted_iota(I32, (block, breadth), 1) >= breadth // 2
    for p in range(slab):
        match = (jnp.broadcast_to(place, (block, size)) - p * block) == rows_of((block, size))
        label = jnp.sum(jnp.where(match, within, 0.0), axis=1, keepdims=True) - 1.0
        labels[p] = jnp.where(right, target, jnp.broadcast_to(label, (block, breadth)))
    for k in range(slab):
        outs[k][pl.ds(planes * run, block), :] = labels[here ^ k]
    for copy in copies:
        copy.wait()


def pair_kernel(sizes, dest_ref, slot_ref, moving_ref, after_ref, *rest):
    tile, capacity = sizes
    outs, sem = rest[:tile], rest[tile]
    planes, height, breadth = moving_ref.shape[1:]
    here = lax.axis_index("tile")
    steps, ranks = [], []
    for s in range(planes):
        steps.append(dest_ref[1, s] ^ here)
        ranks.append(sum(((steps[u] == steps[s]).astype(I32) for u in range(s)), jnp.int32(0)))

        def act(k, s=s):
            rows = pl.ds(pl.multiple_of(ranks[s] * height, height), height)
            pltpu.make_async_copy(moving_ref.at[1, s], outs[k].at[rows], sem.at[s]).start()

        choose(steps[s], 0, tile, act)
    for k in range(tile):
        label = jnp.full((TILE, breadth), -1.0, F32)
        for s in range(planes):
            rank = jnp.where(steps[s] == k, ranks[s], TILE)
            label = jnp.where(rows_of((TILE, breadth)) == rank, slot_ref[1, s].astype(F32), label)
        outs[k][pl.ds(capacity * height, TILE), :] = label
    for s in range(planes):
        pltpu.make_async_copy(
            moving_ref.at[1, s], outs[0].at[pl.ds(0, height)], sem.at[s]
        ).wait()


def route_kernel(sizes, *rest):
    slab, planes, run, breadth = sizes
    ins, outs = rest[:slab], rest[slab : 2 * slab]
    tags, tag_sem, sem = rest[2 * slab :]
    here = lax.axis_index("slab")
    reads = [
        pltpu.make_async_copy(ins[k].at[pl.ds(planes * run, TILE)], tags.at[k], tag_sem.at[k])
        for k in range(slab)
    ]
    for read in reads:
        read.start()
    for k in range(slab):
        reads[k].wait()
        for s in range(planes):
            target = tags[k, s, breadth - 1].astype(I32)
            rows = pl.ds(pl.multiple_of((target % planes) * run, run), run)

            def act(m, k=k, s=s, rows=rows):
                source = ins[k].at[pl.ds(s * run, run)]
                pltpu.make_async_copy(source, outs[m].at[rows], sem.at[k, s]).start()

            choose((target // planes) ^ here, 0, slab, act)
    for k in range(slab):
        for s in range(planes):
            source = ins[k].at[pl.ds(s * run, run)]
            pltpu.make_async_copy(source, outs[0].at[pl.ds(0, run)], sem.at[k, s]).wait()


def label_kernel(sizes, *rest):
    slab, tile, capacity, top = sizes
    ins, outs = rest[:slab], rest[slab:]
    breadth = outs[0].shape[1]
    slab_here, tile_here = lax.axis_index("slab"), lax.axis_index("tile")
    lane = lax.broadcasted_iota(I32, (1, breadth), 1)
    for m in range(tile):
        first = top + (tile_here ^ m) * capacity
        for k in range(slab):
            line = ins[k][pl.ds(first + capacity - 1, 1), :]
            for r in reversed(range(capacity - 1)):
                line = jnp.where(lane < (r + 1) * TILE, ins[k][pl.ds(first + r, 1), :], line)
            outs[m][pl.ds(slab_here ^ k, 1), :] = line


def spectrum_kernel(live_ref, plane_ref, *rest):
    tabs, out_ref = rest[:6], rest[6]

    def body(t, _):
        out_ref[t] = forward(plane_ref[t], tabs[0:2], tabs[2:4], tabs[4:6])
        return 0

    lax.fori_loop(0, live_ref[0], body, 0)


def second_kernel(sizes, live_ref, shift_ref, plane_ref, fixed_ref, *rest):
    tile, capacity = sizes
    tabs, ins = rest[:10], rest[10 : 10 + tile]
    sum_ref, stat_ref = rest[11 + tile : 13 + tile]
    held, tags, anchor, sem, tag_sem = rest[13 + tile :]
    height, breadth = held.shape[1:]
    line = rows_of((TILE, breadth))
    reads = [
        pltpu.make_async_copy(ins[k].at[pl.ds(capacity * height, TILE)], tags.at[k], tag_sem.at[k])
        for k in range(tile)
    ]
    for read in reads:
        read.start()
    for k in range(tile):
        reads[k].wait()
        for r in range(capacity):
            label = tags[k, r, 0].astype(I32)

            @pl.when(label >= 0)
            def _(k=k, r=r, label=label):
                anchor[label] = k * capacity + r

    def fetch(t):
        def act(k):
            rows = pl.ds(pl.multiple_of(anchor[t] % capacity * height, height), height)
            pltpu.make_async_copy(ins[k].at[rows], held.at[t], sem.at[t]).start()

        choose(anchor[t] // capacity, 0, tile, act)

    for t in range(held.shape[0]):
        fetch(t)
        stat_ref[t] = jnp.zeros((TILE, breadth), F32)

    for t in range(held.shape[0]):
        pltpu.make_async_copy(ins[0].at[pl.ds(0, height)], held.at[t], sem.at[t]).wait()

    def body(t, _):
        partner = held[t]
        moving = forward(partner, tabs[0:2], tabs[2:4], tabs[4:6])
        peak = peak_of(fixed_ref[t], moving, tabs[4:6], tabs[6:8], tabs[8:10])
        weight = weight_of(peak)
        moved = rolled(partner, shift_ref[1, 0, t], shift_ref[1, 1, t])
        sum_ref[t] = plane_ref[t] + weight * moved
        stat_ref[t] = jnp.where(line == 0, jnp.broadcast_to(weight, line.shape), peak)
        return 0

    lax.fori_loop(0, live_ref[0], body, 0)


def first_kernel(slab, live_ref, shift_ref, slot_ref, sum_ref, stat_ref, fixed_ref, *rest):
    tabs, ins = rest[:10], rest[10 : 10 + slab]
    send_ref, peak_ref, plane = rest[10 + slab :]
    height, breadth = plane.shape
    run = height // slab
    band = height // PIECES
    here = lax.axis_index("slab")
    line = rows_of((TILE, breadth))
    peak_ref[...] = jnp.zeros_like(peak_ref)

    def body(t, _):
        for k in range(slab):
            rows = pl.ds(pl.multiple_of((here ^ k) * run, run), run)
            plane[rows, :] = ins[k][pl.ds(pl.multiple_of(t * run, run), run), :]
        partner = plane[...]
        moving = forward(partner, tabs[0:2], tabs[2:4], tabs[4:6])
        peak = peak_of(fixed_ref[t], moving, tabs[4:6], tabs[6:8], tabs[8:10])
        weight = weight_of(peak)
        other = stat_ref[t][0:1, 0:1]
        moved = rolled(partner, shift_ref[0, 0, t], shift_ref[0, 1, t])
        merged = (sum_ref[t] + weight * moved) / (1.0 + weight + other)
        peak_ref[t] = jnp.where(line == 0, jnp.broadcast_to(peak, line.shape), stat_ref[t])
        for b in range(PIECES):
            start = pl.multiple_of(slot_ref[0, t * PIECES + b] * band, band)
            send_ref[pl.ds(start, band), :] = merged[b * band : (b + 1) * band]
        return 0

    lax.fori_loop(0, live_ref[0], body, 0)


def gather_kernel(sizes, data_ref, *rest):
    slab, tile, capacity = sizes
    ins, out_ref = rest[:tile], rest[tile]
    tags, tag_sem = rest[tile + 1 :]
    band = out_ref.shape[1]
    tile_here = lax.axis_index("tile")
    reads = [pltpu.make_async_copy(ins[m], tags.at[m], tag_sem.at[m]) for m in range(tile)]
    for read in reads:
        read.start()
    out_ref[...] = jnp.zeros_like(out_ref)
    for read in reads:
        read.wait()

    def add(n, _):
        p, q = n // tile, n % tile
        for r in range(capacity):
            label = tags[q ^ tile_here, p, r * TILE].astype(I32)
            start = pl.multiple_of((n * capacity + r) * band, band)

            @pl.when(label >= 0)
            def _(label=label, start=start):
                out_ref[label] += data_ref[pl.ds(start, band), :]

        return 0

    lax.fori_loop(0, slab * tile, add, 0)


def call(kernel, out_shape, room=4, cost=(1_000_000, 4_000_000), **kwargs):
    return pl.pallas_call(
        kernel,
        out_shape=out_shape,
        compiler_params=pltpu.CompilerParams(vmem_limit_bytes=room << 20),
        cost_estimate=pl.CostEstimate(flops=cost[0], bytes_accessed=cost[1], transcendentals=0),
        **kwargs,
    )


def exchange(arrays, axis):
    size = len(arrays)
    got = [arrays[0]] + [None] * (size - 1)
    for k in reversed(range(1, size)):
        got[k] = lax.ppermute(arrays[k], axis, [(i, i ^ k) for i in range(size)])
    return got


def local(fixed_planes, moving_planes, pair_dest, pair_slot, plane_shift, live_count, piece_block):
    planes, height, breadth = fixed_planes.shape
    slab, tile = lax.axis_size("slab"), lax.axis_size("tile")
    devices = slab * tile
    count = piece_block.shape[0]
    run = height // slab
    band = height // PIECES
    tile_capacity = max(2, (planes + tile - 1) // tile)
    capacity = max(2, (count + devices - 1) // devices)
    block = tile * capacity
    spectrum_rows = height // 2 + PAD
    dma = pltpu.SemaphoreType.DMA
    shape = jax.ShapeDtypeStruct
    tabs = [jnp.asarray(t) for t in tables(height, breadth)]
    moving_planes, pair_dest, pair_slot, plane_shift = [
        pltpu.with_memory_space_constraint(x, pltpu.HBM)
        for x in (moving_planes, pair_dest, pair_slot, plane_shift)
    ]

    spread = call(
        functools.partial(spread_kernel, count, (slab, tile, capacity)),
        [shape((planes * run + block, breadth), F32)] * slab + [shape((TILE, count), I32)],
        in_specs=[VMEM, SMEM, SMEM, SMEM, HBM],
        out_specs=[VMEM] * (slab + 1),
        scratch_shapes=[pltpu.VMEM((slab, block, breadth), F32), dma((slab, planes))],
        name="spread",
    )(piece_block.reshape(1, count), pair_dest, pair_slot, live_count, moving_planes)
    slots = spread[slab]
    runs = exchange(spread[:slab], "slab")

    paired = call(
        functools.partial(pair_kernel, (tile, tile_capacity)),
        [shape((tile_capacity * height + TILE, breadth), F32)] * tile,
        in_specs=[SMEM, SMEM, HBM, VMEM],
        out_specs=[VMEM] * tile,
        scratch_shapes=[dma((planes,))],
        name="pair",
    )(pair_dest, pair_slot, moving_planes, slots)
    second_partners = exchange(paired, "tile")

    spectrum = call(
        spectrum_kernel,
        shape((planes, spectrum_rows, 2 * breadth), F32),
        in_specs=[SMEM] + [VMEM] * 7,
        out_specs=VMEM,
        cost=(10**9, 4 * 10**6),
        name="spectrum",
    )(live_count, fixed_planes, *tabs[:6])

    routed = call(
        functools.partial(route_kernel, (slab, planes, run, breadth)),
        [shape((planes * run, breadth), F32)] * slab,
        in_specs=[VMEM] * slab,
        out_specs=[VMEM] * slab,
        scratch_shapes=[pltpu.SMEM((slab, TILE, breadth), F32), dma((slab,)), dma((slab, planes))],
        name="route",
    )(*runs)
    first_partners = exchange(routed, "slab")

    labels = call(
        functools.partial(label_kernel, (slab, tile, capacity, planes * run)),
        [shape((slab, breadth), F32)] * tile,
        in_specs=[VMEM] * slab,
        out_specs=[VMEM] * tile,
        name="label",
    )(*runs)
    band_labels = exchange(labels, "tile")

    summed, stats = call(
        functools.partial(second_kernel, (tile, tile_capacity)),
        [shape((planes, height, breadth), F32), shape((planes, TILE, breadth), F32)],
        in_specs=[SMEM, SMEM] + [VMEM] * (12 + tile) + [VMEM],
        out_specs=[VMEM, VMEM],
        scratch_shapes=[
            pltpu.VMEM((planes, height, breadth), F32),
            pltpu.SMEM((tile, TILE, breadth), F32),
            pltpu.SMEM((planes,), I32),
            dma((planes,)),
            dma((tile,)),
        ],
        cost=(2 * 10**9, 6 * 10**6),
        room=6,
        name="second",
    )(live_count, plane_shift, fixed_planes, spectrum, *tabs, *second_partners, routed[0])

    send, tops = call(
        functools.partial(first_kernel, slab),
        [shape((devices * capacity * band, breadth), F32), shape((planes, TILE, breadth), F32)],
        in_specs=[SMEM, SMEM, SMEM] + [VMEM] * (13 + slab),
        out_specs=[VMEM, VMEM],
        scratch_shapes=[pltpu.VMEM((height, breadth), F32)],
        cost=(2 * 10**9, 6 * 10**6),
        room=8,
        name="first",
    )(live_count, plane_shift, slots, summed, stats, spectrum, *tabs, *first_partners)

    arrived = lax.all_to_all(
        send.reshape(devices, capacity * band, breadth), ("slab", "tile"), 0, 0, tiled=True
    )
    blocks = call(
        functools.partial(gather_kernel, (slab, tile, capacity)),
        shape((OWNED, band, breadth), F32),
        in_specs=[VMEM] * (tile + 1),
        out_specs=VMEM,
        scratch_shapes=[pltpu.SMEM((tile, slab, breadth), F32), dma((tile,))],
        room=8,
        name="gather",
    )(arrived.reshape(devices * capacity * band, breadth), *band_labels)
    return (jnp.transpose(tops[:, :2, 0]), blocks)


def solution(mesh):
    placed = (
        P(("slab", "tile"), None, None),
        P(None, ("slab", "tile"), None, None),
        P(None, ("slab", "tile")),
        P(None, ("slab", "tile")),
        P(None, None, ("slab", "tile")),
        P(("slab", "tile")),
        P(("slab", "tile")),
    )
    return jax.shard_map(
        local,
        mesh=mesh,
        in_specs=placed,
        out_specs=(P(None, ("slab", "tile")), P(("slab", "tile"), None, None)),
        check_vma=False,
    )
```

profile of v0, /device:TPU:0, one launch (start us, length us, event | category | flops | bytes accessed | tf_op | source)
XLA Modules:
  0.0 116.5 jit_solution(12746580091638244948)
XLA Ops:
  1.9 2.2 %spread.1 = (f32[264,128]{1,0:T(8,128)S(1)}, f32[264,128]{1,0:T(8,128)S(1)}, f32[264,128]{1,0:T(8,128)S(1)}, f32[264,128]{1,0:T(8,128)S(1)}, f32[264,128]{1,0:T(...) custom-call(s32[1,64]{1,0:T(1,128)S(1)} %bitcast.7, ...), custom_call_target="tpu_custom_call" | custom-call | flops 1000000 | bytes 4000000 | tf_op jit(solution)/shard_map/spread/pallas_call | solution.py:415
  4.2 3.0 %collective-permute-start.3 = (f32[264,128]{1,0:T(8,128)S(1)}, f32[264,128]{1,0:T(8,128)S(1)}, u32[]{:S(2)}, u32[]{:S(2)}) collective-permute-start(f32[264,128]{1,0:T(8,128)S(1)} %get-tuple-element.37), channel_id=1, source_target_pairs={{0,4},{4,0},{8,12},{12,8},{16,20},{20,16},{24,28},{28,24},{1,5},{5... | collective-permute-start | bytes 405512 | tf_op jit(solution)/shard_map/ppermute | solution.py:392
  8.8 1.9 %pair.1 = (f32[1032,128]{1,0:T(8,128)S(1)}, f32[1032,128]{1,0:T(8,128)S(1)}, f32[1032,128]{1,0:T(8,128)S(1)}, f32[1032,128]{1,0:T(8,128)S(1)}) custom-call(s32[2,4]{1,0:T(2,128)} %dest_ref.3, s32[2,4]{1,0:T(2,128)} %slot_ref.3, f32[2,4,512,128]{3,2,1,0:T(8,128)} %moving_ref.3, s32[8,64]{1,0:T(8,128)S(1)} %get-tuple-element.31.after_ref.slot_ref), custom_call_target="tpu_custom_call" | custom-call | flops 1000000 | bytes 4000000 | tf_op jit(solution)/shard_map/pair/pallas_call | solution.py:426
  10.9 2.0 %collective-permute-start.1 = (f32[1032,128]{1,0:T(8,128)S(1)}, f32[1032,128]{1,0:T(8,128)S(1)}, u32[]{:S(2)}, u32[]{:S(2)}) collective-permute-start(f32[1032,128]{1,0:T(8,128)S(1)} %get-tuple-element.34), channel_id=1, source_target_pairs={{0,2},{1,3},{2,0},{3,1},{4,6},{5,7},{6,4},{7,5},{8,10},{9,11},{10,... | collective-permute-start | bytes 1585160 | tf_op jit(solution)/shard_map/ppermute | solution.py:392
  13.7 2.6 %collective-permute-start.6 = (f32[264,128]{1,0:T(8,128)S(1)}, f32[264,128]{1,0:T(8,128)S(1)}, u32[]{:S(2)}, u32[]{:S(2)}) collective-permute-start(f32[264,128]{1,0:T(8,128)S(1)} %get-tuple-element.40), channel_id=1, source_target_pairs={{0,16},{4,20},{8,24},{12,28},{16,0},{20,4},{24,8},{28,12},{1,17},{... | collective-permute-start | bytes 405512 | tf_op jit(solution)/shard_map/ppermute | solution.py:392
  16.3 2.4 %collective-permute-start.7 = (f32[264,128]{1,0:T(8,128)S(1)}, f32[264,128]{1,0:T(8,128)S(1)}, u32[]{:S(2)}, u32[]{:S(2)}) collective-permute-start(f32[264,128]{1,0:T(8,128)S(1)} %get-tuple-element.41), channel_id=1, source_target_pairs={{0,20},{4,16},{8,28},{12,24},{16,4},{20,0},{24,12},{28,8},{1,21},{... | collective-permute-start | bytes 405512 | tf_op jit(solution)/shard_map/ppermute | solution.py:392
  18.7 8.1 %collective-permute-done.6.rest_4_ = f32[264,128]{1,0:T(8,128)S(1)} collective-permute-done((f32[264,128]{1,0:T(8,128)S(1)}, f32[264,128]{1,0:T(8,128)S(1)}, u32[]{:S(2)}, u32[]{:S(2)}) %collective-permute-start.6) | collective-permute-done | bytes 135200 | tf_op jit(solution)/shard_map/ppermute | solution.py:392
  26.8 2.5 %collective-permute-start.8 = (f32[264,128]{1,0:T(8,128)S(1)}, f32[264,128]{1,0:T(8,128)S(1)}, u32[]{:S(2)}, u32[]{:S(2)}) collective-permute-start(f32[264,128]{1,0:T(8,128)S(1)} %get-tuple-element.42), channel_id=1, source_target_pairs={{0,24},{4,28},{8,16},{12,20},{16,8},{20,12},{24,0},{28,4},{1,25},{... | collective-permute-start | bytes 405512 | tf_op jit(solution)/shard_map/ppermute | solution.py:392
  29.7 3.4 %collective-permute-start.9 = (f32[264,128]{1,0:T(8,128)S(1)}, f32[264,128]{1,0:T(8,128)S(1)}, u32[]{:S(2)}, u32[]{:S(2)}) collective-permute-start(f32[264,128]{1,0:T(8,128)S(1)} %get-tuple-element.43), channel_id=1, source_target_pairs={{0,28},{4,24},{8,20},{12,16},{16,12},{20,8},{24,4},{28,0},{1,29},{... | collective-permute-start | bytes 405512 | tf_op jit(solution)/shard_map/ppermute | solution.py:392
  33.7 3.7 %collective-permute-done.9.rest_7_ = f32[264,128]{1,0:T(8,128)S(1)} collective-permute-done((f32[264,128]{1,0:T(8,128)S(1)}, f32[264,128]{1,0:T(8,128)S(1)}, u32[]{:S(2)}, u32[]{:S(2)}) %collective-permute-start.9) | collective-permute-done | bytes 135200 | tf_op jit(solution)/shard_map/ppermute | solution.py:392
  37.4 3.5 %route.1 = (f32[256,128]{1,0:T(8,128)S(1)}, f32[256,128]{1,0:T(8,128)S(1)}, f32[256,128]{1,0:T(8,128)S(1)}, f32[256,128]{1,0:T(8,128)S(1)}, f32[256,128]{1,0:T(8...) custom-call(f32[264,128]{1,0:T(8,128)S(1)} %get-tuple-element.36.rest_0_, ...), custom_call_target="tpu_custom_call" | custom-call | flops 1000000 | bytes 4000000 | tf_op jit(solution)/shard_map/route/pallas_call | solution.py:445
  42.4 3.6 %collective-permute-start.11 = (f32[256,128]{1,0:T(8,128)S(1)}, f32[256,128]{1,0:T(8,128)S(1)}, u32[]{:S(2)}, u32[]{:S(2)}) collective-permute-start(f32[256,128]{1,0:T(8,128)S(1)} %get-tuple-element.48), channel_id=1, source_target_pairs={{0,8},{4,12},{8,0},{12,4},{16,24},{20,28},{24,16},{28,20},{1,9},{5... | collective-permute-start | bytes 393224 | tf_op jit(solution)/shard_map/ppermute | solution.py:392
  47.2 3.7 %collective-permute-start.12 = (f32[256,128]{1,0:T(8,128)S(1)}, f32[256,128]{1,0:T(8,128)S(1)}, u32[]{:S(2)}, u32[]{:S(2)}) collective-permute-start(f32[256,128]{1,0:T(8,128)S(1)} %get-tuple-element.49), channel_id=1, source_target_pairs={{0,12},{4,8},{8,4},{12,0},{16,28},{20,24},{24,20},{28,16},{1,13},{... | collective-permute-start | bytes 393224 | tf_op jit(solution)/shard_map/ppermute | solution.py:392
  50.9 2.1 %collective-permute-start.13 = (f32[256,128]{1,0:T(8,128)S(1)}, f32[256,128]{1,0:T(8,128)S(1)}, u32[]{:S(2)}, u32[]{:S(2)}) collective-permute-start(f32[256,128]{1,0:T(8,128)S(1)} %get-tuple-element.50), channel_id=1, source_target_pairs={{0,16},{4,20},{8,24},{12,28},{16,0},{20,4},{24,8},{28,12},{1,17},{... | collective-permute-start | bytes 393224 | tf_op jit(solution)/shard_map/ppermute | solution.py:392
  54.1 4.0 %collective-permute-start.15 = (f32[256,128]{1,0:T(8,128)S(1)}, f32[256,128]{1,0:T(8,128)S(1)}, u32[]{:S(2)}, u32[]{:S(2)}) collective-permute-start(f32[256,128]{1,0:T(8,128)S(1)} %get-tuple-element.52), channel_id=1, source_target_pairs={{0,24},{4,28},{8,16},{12,20},{16,8},{20,12},{24,0},{28,4},{1,25},{... | collective-permute-start | bytes 393224 | tf_op jit(solution)/shard_map/ppermute | solution.py:392
  58.6 4.4 %second.1 = (f32[4,512,128]{2,1,0:T(8,128)S(1)}, f32[4,8,128]{2,1,0:T(8,128)S(1)}) custom-call(s32[1]{0:T(128)S(6)} %copy.20.live_ref, s32[2,2,4]{2,1,0:T(2,128)} %shift_ref.3, f32[4,512,128]{2,1,0:T(8,128)S(1)} %copy-done.1, f32[4,272,256]{2,1,0:T(8,128)S(1)} %spectrum.1.fixed_ref, bf16[256,256]{1,0:T(8,128)(2,1)S(1)} %copy-done.7, ...), custom_call_target="tpu_custom_call" | custom-call | flops 2000000000 | bytes 6000000 | tf_op jit(solution)/shard_map/second/pallas_call | solution.py:464
  63.0 6.2 %collective-permute-done.13.rest_14_ = f32[256,128]{1,0:T(8,128)S(1)} collective-permute-done((f32[256,128]{1,0:T(8,128)S(1)}, f32[256,128]{1,0:T(8,128)S(1)}, u32[]{:S(2)}, u32[]{:S(2)}) %collective-permute-start.13) | collective-permute-done | bytes 131104 | tf_op jit(solution)/shard_map/ppermute | solution.py:392
  69.2 2.9 %collective-permute-done.14.rest_15_ = f32[256,128]{1,0:T(8,128)S(1)} collective-permute-done((f32[256,128]{1,0:T(8,128)S(1)}, f32[256,128]{1,0:T(8,128)S(1)}, u32[]{:S(2)}, u32[]{:S(2)}) %collective-permute-start.14) | collective-permute-done | bytes 131104 | tf_op jit(solution)/shard_map/ppermute | solution.py:392
  72.0 4.5 %first.1 = (f32[2048,128]{1,0:T(8,128)}, f32[4,8,128]{2,1,0:T(8,128)S(1)}) custom-call(s32[1]{0:T(128)S(6)} %copy.20.live_ref, s32[2,2,4]{2,1,0:T(2,128)} %shift_ref.3, s32[8,64]{1,0:T(8,128)S(1)} %get-tuple-element.31.after_ref.slot_ref, f32[4,512,128]{2,1,0:T(8,128)S(1)} %get-tuple-element.45.sum_ref, f32[4,8,128]{2,1,0:T(8,128)S(1)} %get-tuple-element.46.stat_ref, ...), custom_call_target="tpu_custom_call" | custom-call | flops 2000000000 | bytes 6000000 | tf_op jit(solution)/shard_map/first/pallas_call | solution.py:481
  76.6 11.1 %all-to-all-start = ((f32[32,64,128]{2,1,0:T(8,128)}), f32[32,64,128]{2,1,0:T(8,128)S(1)}, u32[]{:S(2)}, u32[]{:S(2)}) async-start(f32[32,64,128]{2,1,0:T(8,128)} %bitcast.3), calls=%async_computation | async-start | bytes 2097152 | tf_op jit(solution)/shard_map/all_to_all | solution.py:492
  88.0 1.6 %collective-permute-start.18 = (f32[8,128]{1,0:T(8,128)S(1)}, f32[8,128]{1,0:T(8,128)S(1)}, u32[]{:S(2)}, u32[]{:S(2)}) collective-permute-start(f32[8,128]{1,0:T(8,128)S(1)} %get-tuple-element.58), channel_id=1, source_target_pairs={{0,2},{1,3},{2,0},{3,1},{4,6},{5,7},{6,4},{7,5},{8,10},{9,11},{10,... | collective-permute-start | bytes 12296 | tf_op jit(solution)/shard_map/ppermute | solution.py:392
  90.3 2.1 %collective-permute-done.18.rest_2_ = f32[8,128]{1,0:T(8,128)S(1)} collective-permute-done((f32[8,128]{1,0:T(8,128)S(1)}, f32[8,128]{1,0:T(8,128)S(1)}, u32[]{:S(2)}, u32[]{:S(2)}) %collective-permute-start.18) | collective-permute-done | bytes 4128 | tf_op jit(solution)/shard_map/ppermute | solution.py:392
  92.8 21.1 %all-to-all-done = f32[32,64,128]{2,1,0:T(8,128)S(1)} async-done(((f32[32,64,128]{2,1,0:T(8,128)}), f32[32,64,128]{2,1,0:T(8,128)S(1)}, u32[]{:S(2)}, u32[]{:S(2)}) %all-to-all-start) | async-done | bytes 1048608 | tf_op jit(solution)/shard_map/all_to_all | solution.py:492
  113.9 2.7 %gather.1 = f32[16,32,128]{2,1,0:T(8,128)} custom-call(f32[2048,128]{1,0:T(8,128)S(1)} %bitcast.6, f32[8,128]{1,0:T(8,128)S(1)} %get-tuple-element.56.rest_0_, f32[8,128]{1,0:T(8,128)S(1)} %collective-permute-done.17.rest_1_, f32[8,128]{1,0:T(8,128)S(1)} %collective-permute-done.18.rest_2_, f32[8,128]{1,0:T(8,128)S(1)} %collective-permute-done.19.rest_3_), custom_call_target="tpu_custom_call" | custom-call | flops 1000000 | bytes 4000000 | tf_op jit(solution)/shard_map/gather/pallas_call | solution.py:495
  (52 shorter events, 9.7 us)
Async XLA Ops:
  4.2 41.8 %copy-start.1 = (f32[4,512,128]{2,1,0:T(8,128)S(1)}, f32[4,512,128]{2,1,0:T(8,128)}, u32[]{:S(2)}) copy-start(f32[4,512,128]{2,1,0:T(8,128)} %plane_ref.3) | copy-start | bytes 3145732
  4.2 41.8 %copy-start.2 = (bf16[256,256]{1,0:T(8,128)(2,1)S(1)}, bf16[256,256]{1,0:T(8,128)(2,1)}, u32[]{:S(2)}) copy-start(bf16[256,256]{1,0:T(8,128)(2,1)} %constant.25.clone.rest_5_) | copy-start | bytes 393220
  4.2 41.8 %copy-start.3 = (bf16[256,256]{1,0:T(8,128)(2,1)S(1)}, bf16[256,256]{1,0:T(8,128)(2,1)}, u32[]{:S(2)}) copy-start(bf16[256,256]{1,0:T(8,128)(2,1)} %constant.24.clone.rest_4_) | copy-start | bytes 393220
  4.2 8.6 %collective-permute-start.3 = (f32[264,128]{1,0:T(8,128)S(1)}, f32[264,128]{1,0:T(8,128)S(1)}, u32[]{:S(2)}, u32[]{:S(2)}) collective-permute-start(f32[264,128]{1,0:T(8,128)S(1)} %get-tuple-element.37), channel_id=1, source_target_pairs={{0,4},{4,0},{8,12},{12,8},{16,20},{20,16},{24,28},{28,24},{1,5},{5... | collective-permute-start | bytes 405512 | tf_op jit(solution)/shard_map/ppermute | solution.py:392
  7.3 6.5 %collective-permute-start.4 = (f32[264,128]{1,0:T(8,128)S(1)}, f32[264,128]{1,0:T(8,128)S(1)}, u32[]{:S(2)}, u32[]{:S(2)}) collective-permute-start(f32[264,128]{1,0:T(8,128)S(1)} %get-tuple-element.38), channel_id=1, source_target_pairs={{0,8},{4,12},{8,0},{12,4},{16,24},{20,28},{24,16},{28,20},{1,9},{5... | collective-permute-start | bytes 405512 | tf_op jit(solution)/shard_map/ppermute | solution.py:392
  8.8 7.5 %collective-permute-start.5 = (f32[264,128]{1,0:T(8,128)S(1)}, f32[264,128]{1,0:T(8,128)S(1)}, u32[]{:S(2)}, u32[]{:S(2)}) collective-permute-start(f32[264,128]{1,0:T(8,128)S(1)} %get-tuple-element.39), channel_id=1, source_target_pairs={{0,12},{4,8},{8,4},{12,0},{16,28},{20,24},{24,20},{28,16},{1,13},{... | collective-permute-start | bytes 405512 | tf_op jit(solution)/shard_map/ppermute | solution.py:392
  10.8 42.2 %collective-permute-start = (f32[1032,128]{1,0:T(8,128)S(1)}, f32[1032,128]{1,0:T(8,128)S(1)}, u32[]{:S(2)}, u32[]{:S(2)}) collective-permute-start(f32[1032,128]{1,0:T(8,128)S(1)} %get-tuple-element.33), channel_id=1, source_target_pairs={{0,1},{1,0},{2,3},{3,2},{4,5},{5,4},{6,7},{7,6},{8,9},{9,8},{10,11... | collective-permute-start | bytes 1585160 | tf_op jit(solution)/shard_map/ppermute | solution.py:392
  10.9 43.2 %collective-permute-start.1 = (f32[1032,128]{1,0:T(8,128)S(1)}, f32[1032,128]{1,0:T(8,128)S(1)}, u32[]{:S(2)}, u32[]{:S(2)}) collective-permute-start(f32[1032,128]{1,0:T(8,128)S(1)} %get-tuple-element.34), channel_id=1, source_target_pairs={{0,2},{1,3},{2,0},{3,1},{4,6},{5,7},{6,4},{7,5},{8,10},{9,11},{10,... | collective-permute-start | bytes 1585160 | tf_op jit(solution)/shard_map/ppermute | solution.py:392
  12.9 45.2 %collective-permute-start.2 = (f32[1032,128]{1,0:T(8,128)S(1)}, f32[1032,128]{1,0:T(8,128)S(1)}, u32[]{:S(2)}, u32[]{:S(2)}) collective-permute-start(f32[1032,128]{1,0:T(8,128)S(1)} %get-tuple-element.35), channel_id=1, source_target_pairs={{0,3},{1,2},{2,1},{3,0},{4,7},{5,6},{6,5},{7,4},{8,11},{9,10},{10,... | collective-permute-start | bytes 1585160 | tf_op jit(solution)/shard_map/ppermute | solution.py:392
  13.7 13.1 %collective-permute-start.6 = (f32[264,128]{1,0:T(8,128)S(1)}, f32[264,128]{1,0:T(8,128)S(1)}, u32[]{:S(2)}, u32[]{:S(2)}) collective-permute-start(f32[264,128]{1,0:T(8,128)S(1)} %get-tuple-element.40), channel_id=1, source_target_pairs={{0,16},{4,20},{8,24},{12,28},{16,0},{20,4},{24,8},{28,12},{1,17},{... | collective-permute-start | bytes 405512 | tf_op jit(solution)/shard_map/ppermute | solution.py:392
  16.3 13.3 %collective-permute-start.7 = (f32[264,128]{1,0:T(8,128)S(1)}, f32[264,128]{1,0:T(8,128)S(1)}, u32[]{:S(2)}, u32[]{:S(2)}) collective-permute-start(f32[264,128]{1,0:T(8,128)S(1)} %get-tuple-element.41), channel_id=1, source_target_pairs={{0,20},{4,16},{8,28},{12,24},{16,4},{20,0},{24,12},{28,8},{1,21},{... | collective-permute-start | bytes 405512 | tf_op jit(solution)/shard_map/ppermute | solution.py:392
  26.8 6.9 %collective-permute-start.8 = (f32[264,128]{1,0:T(8,128)S(1)}, f32[264,128]{1,0:T(8,128)S(1)}, u32[]{:S(2)}, u32[]{:S(2)}) collective-permute-start(f32[264,128]{1,0:T(8,128)S(1)} %get-tuple-element.42), channel_id=1, source_target_pairs={{0,24},{4,28},{8,16},{12,20},{16,8},{20,12},{24,0},{28,4},{1,25},{... | collective-permute-start | bytes 405512 | tf_op jit(solution)/shard_map/ppermute | solution.py:392
  29.7 7.7 %collective-permute-start.9 = (f32[264,128]{1,0:T(8,128)S(1)}, f32[264,128]{1,0:T(8,128)S(1)}, u32[]{:S(2)}, u32[]{:S(2)}) collective-permute-start(f32[264,128]{1,0:T(8,128)S(1)} %get-tuple-element.43), channel_id=1, source_target_pairs={{0,28},{4,24},{8,20},{12,16},{16,12},{20,8},{24,4},{28,0},{1,29},{... | collective-permute-start | bytes 405512 | tf_op jit(solution)/shard_map/ppermute | solution.py:392
  41.0 6.2 %collective-permute-start.10 = (f32[256,128]{1,0:T(8,128)S(1)}, f32[256,128]{1,0:T(8,128)S(1)}, u32[]{:S(2)}, u32[]{:S(2)}) collective-permute-start(f32[256,128]{1,0:T(8,128)S(1)} %get-tuple-element.47), channel_id=1, source_target_pairs={{0,4},{4,0},{8,12},{12,8},{16,20},{20,16},{24,28},{28,24},{1,5},{5... | collective-permute-start | bytes 393224 | tf_op jit(solution)/shard_map/ppermute | solution.py:392
  42.4 8.5 %collective-permute-start.11 = (f32[256,128]{1,0:T(8,128)S(1)}, f32[256,128]{1,0:T(8,128)S(1)}, u32[]{:S(2)}, u32[]{:S(2)}) collective-permute-start(f32[256,128]{1,0:T(8,128)S(1)} %get-tuple-element.48), channel_id=1, source_target_pairs={{0,8},{4,12},{8,0},{12,4},{16,24},{20,28},{24,16},{28,20},{1,9},{5... | collective-permute-start | bytes 393224 | tf_op jit(solution)/shard_map/ppermute | solution.py:392
  47.2 15.8 %collective-permute-start.12 = (f32[256,128]{1,0:T(8,128)S(1)}, f32[256,128]{1,0:T(8,128)S(1)}, u32[]{:S(2)}, u32[]{:S(2)}) collective-permute-start(f32[256,128]{1,0:T(8,128)S(1)} %get-tuple-element.49), channel_id=1, source_target_pairs={{0,12},{4,8},{8,4},{12,0},{16,28},{20,24},{24,20},{28,16},{1,13},{... | collective-permute-start | bytes 393224 | tf_op jit(solution)/shard_map/ppermute | solution.py:392
  50.9 18.3 %collective-permute-start.13 = (f32[256,128]{1,0:T(8,128)S(1)}, f32[256,128]{1,0:T(8,128)S(1)}, u32[]{:S(2)}, u32[]{:S(2)}) collective-permute-start(f32[256,128]{1,0:T(8,128)S(1)} %get-tuple-element.50), channel_id=1, source_target_pairs={{0,16},{4,20},{8,24},{12,28},{16,0},{20,4},{24,8},{28,12},{1,17},{... | collective-permute-start | bytes 393224 | tf_op jit(solution)/shard_map/ppermute | solution.py:392
  53.0 19.0 %collective-permute-start.14 = (f32[256,128]{1,0:T(8,128)S(1)}, f32[256,128]{1,0:T(8,128)S(1)}, u32[]{:S(2)}, u32[]{:S(2)}) collective-permute-start(f32[256,128]{1,0:T(8,128)S(1)} %get-tuple-element.51), channel_id=1, source_target_pairs={{0,20},{4,16},{8,28},{12,24},{16,4},{20,0},{24,12},{28,8},{1,21},{... | collective-permute-start | bytes 393224 | tf_op jit(solution)/shard_map/ppermute | solution.py:392
  54.1 17.9 %collective-permute-start.15 = (f32[256,128]{1,0:T(8,128)S(1)}, f32[256,128]{1,0:T(8,128)S(1)}, u32[]{:S(2)}, u32[]{:S(2)}) collective-permute-start(f32[256,128]{1,0:T(8,128)S(1)} %get-tuple-element.52), channel_id=1, source_target_pairs={{0,24},{4,28},{8,16},{12,20},{16,8},{20,12},{24,0},{28,4},{1,25},{... | collective-permute-start | bytes 393224 | tf_op jit(solution)/shard_map/ppermute | solution.py:392
  58.1 13.9 %collective-permute-start.16 = (f32[256,128]{1,0:T(8,128)S(1)}, f32[256,128]{1,0:T(8,128)S(1)}, u32[]{:S(2)}, u32[]{:S(2)}) collective-permute-start(f32[256,128]{1,0:T(8,128)S(1)} %get-tuple-element.53), channel_id=1, source_target_pairs={{0,28},{4,24},{8,20},{12,16},{16,12},{20,8},{24,4},{28,0},{1,29},{... | collective-permute-start | bytes 393224 | tf_op jit(solution)/shard_map/ppermute | solution.py:392
  76.6 37.3 %all-to-all-start = ((f32[32,64,128]{2,1,0:T(8,128)}), f32[32,64,128]{2,1,0:T(8,128)S(1)}, u32[]{:S(2)}, u32[]{:S(2)}) async-start(f32[32,64,128]{2,1,0:T(8,128)} %bitcast.3), calls=%async_computation | async-start | bytes 2097152 | tf_op jit(solution)/shard_map/all_to_all | solution.py:492
  87.7 2.6 %collective-permute-start.17 = (f32[8,128]{1,0:T(8,128)S(1)}, f32[8,128]{1,0:T(8,128)S(1)}, u32[]{:S(2)}, u32[]{:S(2)}) collective-permute-start(f32[8,128]{1,0:T(8,128)S(1)} %get-tuple-element.57), channel_id=1, source_target_pairs={{0,1},{1,0},{2,3},{3,2},{4,5},{5,4},{6,7},{7,6},{8,9},{9,8},{10,11... | collective-permute-start | bytes 12296 | tf_op jit(solution)/shard_map/ppermute | solution.py:392
  88.0 4.4 %collective-permute-start.18 = (f32[8,128]{1,0:T(8,128)S(1)}, f32[8,128]{1,0:T(8,128)S(1)}, u32[]{:S(2)}, u32[]{:S(2)}) collective-permute-start(f32[8,128]{1,0:T(8,128)S(1)} %get-tuple-element.58), channel_id=1, source_target_pairs={{0,2},{1,3},{2,0},{3,1},{4,6},{5,7},{6,4},{7,5},{8,10},{9,11},{10,... | collective-permute-start | bytes 12296 | tf_op jit(solution)/shard_map/ppermute | solution.py:392
  89.6 3.1 %collective-permute-start.19 = (f32[8,128]{1,0:T(8,128)S(1)}, f32[8,128]{1,0:T(8,128)S(1)}, u32[]{:S(2)}, u32[]{:S(2)}) collective-permute-start(f32[8,128]{1,0:T(8,128)S(1)} %get-tuple-element.59), channel_id=1, source_target_pairs={{0,3},{1,2},{2,1},{3,0},{4,7},{5,6},{6,5},{7,4},{8,11},{9,10},{10,... | collective-permute-start | bytes 12296 | tf_op jit(solution)/shard_map/ppermute | solution.py:392
  (9 other events, 238.4 us)
where the time goes:
time: 117 us
  starting transfers between devices  47 us (40%)
  waiting for transfers between devices  46.3 us (40%)
  Pallas kernels  20.4 us (17%)
  between operations  1.51 us (1%)
  local copies, waits for them, and re-layouts  1.38 us (1%)
    ppermute x20, starting transfers between devices, exchange(): got[k] = lax.ppermute(arrays[k], axis, [(i, i ^ k) for i in range(size)])  35.9 us
    ppermute x20, waiting for transfers between devices, exchange(): got[k] = lax.ppermute(arrays[k], axis, [(i, i ^ k) for i in range(size)])  25.2 us
    all_to_all x1, waiting for transfers between devices, local(): lax.all_to_all(send.reshape(devices, capacity * band, breadth), ('slab',...  21.1 us
    all_to_all x1, starting transfers between devices, local(): lax.all_to_all(send.reshape(devices, capacity * band, breadth), ('slab',...  11.1 us
    pallas_call x1, Pallas kernels, local(): call(functools.partial(first_kernel, slab), [shape((devices * capacity *...  4.54 us
    pallas_call x1, Pallas kernels, local(): call(functools.partial(second_kernel, (tile, tile_capacity)), [shape((pla...  4.4 us
    pallas_call x1, Pallas kernels, local(): call(functools.partial(route_kernel, (slab, planes, run, breadth)), [shap...  3.51 us
    pallas_call x1, Pallas kernels, local(): call(functools.partial(gather_kernel, (slab, tile, capacity)), shape((OWN...  2.67 us
  transfers between devices with their start and end apart: 21, of which 10 were waited for; matrix products, arithmetic and copies ran while one was open for 1% of the time, Pallas kernels for 9%

commit v1 on v0

--- a/solution.py
+++ b/solution.py
@@ -62,11 +62,17 @@
     return jnp.dot(a, b, preferred_element_type=F32)
 
 
-def table_times(high, low, x):
-    x_high, x_low = split(x)
-    breadth = x.shape[1]
-    both = dot(high[...], jnp.concatenate([x_high, x_low], 1))
-    return both[:, :breadth] + both[:, breadth:] + dot(low[...], x_high)
+def table_times(high, low, xs):
+    parts = [split(x) for x in xs]
+    breadth = xs[0].shape[1]
+    shared = dot(low[...], jnp.concatenate([part[0] for part in parts], 1))
+    sums = []
+    for n, part in enumerate(parts):
+        both = dot(high[...], jnp.concatenate(part, 1))
+        sums.append(
+            both[:, :breadth] + both[:, breadth:] + shared[:, n * breadth : (n + 1) * breadth]
+        )
+    return sums
 
 
 def times_table(x, high, low):
@@ -78,43 +84,50 @@
     return lax.broadcasted_iota(I32, shape, 0)
 
 
-def forward(x, even, odd, across):
-    height, breadth = x.shape
+def forward(xs, even, odd, across):
+    height, breadth = xs[0].shape
     half, quarter = height // 2, height // 4
-    top, bottom = x[:half], x[half:]
-    e = table_times(*even, top + bottom)
-    o = table_times(*odd, top - bottom)
     first = rows_of((quarter, breadth)) == 0
-    sine = e[quarter:]
-    last = jnp.where(rows_of((PAD, breadth)) == 0, sine[:PAD], 0.0)
-    mixed = jnp.concatenate(
-        [
-            jnp.concatenate([e[:quarter], jnp.where(first, 0.0, sine)], 1),
-            jnp.concatenate([o[:quarter], o[quarter:]], 1),
-            jnp.concatenate([last, jnp.zeros_like(last)], 1),
-        ],
-        0,
-    )
-    return times_table(mixed, *across)
-
-
-def peak_of(fixed, moving, across, even, odd):
-    breadth = fixed.shape[1] // 2
-    half = fixed.shape[0] - PAD
+    evens = table_times(*even, [x[:half] + x[half:] for x in xs])
+    odds = table_times(*odd, [x[:half] - x[half:] for x in xs])
+    spectra = []
+    for e, o in zip(evens, odds):
+        sine = e[quarter:]
+        last = jnp.where(rows_of((PAD, breadth)) == 0, sine[:PAD], 0.0)
+        mixed = jnp.concatenate(
+            [
+                jnp.concatenate([e[:quarter], jnp.where(first, 0.0, sine)], 1),
+                jnp.concatenate([o[:quarter], o[quarter:]], 1),
+                jnp.concatenate([last, jnp.zeros_like(last)], 1),
+            ],
+            0,
+        )
+        spectra.append(times_table(mixed, *across))
+    return spectra
+
+
+def peaks_of(fixed, moving, across, even, odd):
+    breadth = fixed[0].shape[1] // 2
+    half = fixed[0].shape[0] - PAD
     quarter = half // 2
-    fr, fi = fixed[:, :breadth], fixed[:, breadth:]
-    gr, gi = moving[:, :breadth], moving[:, breadth:]
-    real = fr * gr + fi * gi
-    minus = fr * gi - fi * gr
-    factor = lax.rsqrt(real * real + minus * minus + FLOOR**2)
-    v = times_table(jnp.concatenate([real * factor, minus * factor], 1), *across)
-    vr, vn = v[:, :breadth], v[:, breadth:]
     first = rows_of((quarter, breadth)) == 0
-    last = jnp.broadcast_to(vr[half : half + 1], (quarter, breadth))
-    e = table_times(*even, jnp.concatenate([vr[:quarter], jnp.where(first, last, vn[:quarter])], 0))
-    o = table_times(*odd, jnp.concatenate([vr[quarter:half], vn[quarter:half]], 0))
-    highest = e + jnp.abs(o)
-    return jnp.max(jnp.max(highest, axis=0, keepdims=True), axis=1, keepdims=True)
+    lower, upper = [], []
+    for f, g in zip(fixed, moving):
+        fr, fi = f[:, :breadth], f[:, breadth:]
+        gr, gi = g[:, :breadth], g[:, breadth:]
+        real = fr * gr + fi * gi
+        minus = fr * gi - fi * gr
+        factor = lax.rsqrt(real * real + minus * minus + FLOOR**2)
+        v = times_table(jnp.concatenate([real * factor, minus * factor], 1), *across)
+        vr, vn = v[:, :breadth], v[:, breadth:]
+        last = jnp.broadcast_to(vr[half : half + 1], (quarter, breadth))
+        lower.append(jnp.concatenate([vr[:quarter], jnp.where(first, last, vn[:quarter])], 0))
+        upper.append(jnp.concatenate([vr[quarter:half], vn[quarter:half]], 0))
+    peaks = []
+    for e, o in zip(table_times(*even, lower), table_times(*odd, upper)):
+        highest = jnp.max(e + jnp.abs(o), axis=0, keepdims=True)
+        peaks.append(jnp.max(highest, axis=1, keepdims=True))
+    return peaks
 
 
 def weight_of(peak):
@@ -142,22 +155,39 @@
         choose(value, middle, high, act)
 
 
-def spread_kernel(count, sizes, pieces_ref, dest_ref, slot_ref, live_ref, moving_ref, *rest):
+def spread_kernel(count, sizes, pieces_hbm, dest_hbm, slot_hbm, live_hbm, moving_ref, *rest):
     slab, tile, capacity = sizes
-    outs, slots_ref = rest[:slab], rest[slab]
-    labels, sem = rest[slab + 1 :]
+    outs, slots_ref, live_out = rest[:slab], rest[slab], rest[slab + 1]
+    pieces_ref, dest_ref, slot_ref, live_ref, labels, small_sem, sem = rest[slab + 2 :]
     planes, height, breadth = moving_ref.shape[1:]
     run = height // slab
     here = lax.axis_index("slab")
+    small = [
+        pltpu.make_async_copy(source, target, small_sem.at[n])
+        for n, (source, target) in enumerate(
+            (
+                (pieces_hbm, pieces_ref),
+                (dest_hbm, dest_ref),
+                (slot_hbm, slot_ref),
+                (live_hbm, live_ref),
+            )
+        )
+    ]
+    for copy in small:
+        copy.start()
     copies = []
     for k in reversed(range(slab)):
         rows = pl.ds(pl.multiple_of((here ^ k) * run, run), run)
-        for s in range(planes):
-            copy = pltpu.make_async_copy(
-                moving_ref.at[0, s, rows], outs[k].at[pl.ds(s * run, run)], sem.at[k, s]
-            )
-            copy.start()
-            copies.append(copy)
+        copy = pltpu.make_async_copy(
+            moving_ref.at[0, :, rows, :],
+            outs[k].at[pl.ds(0, planes * run)].reshape(planes, run, breadth),
+            sem.at[k],
+        )
+        copy.start()
+        copies.append(copy)
+    for copy in small:
+        copy.wait()
+    live_out[0] = live_ref[0, 0]
     pieces = pieces_ref[...]
     size = count
     row = jnp.broadcast_to(pieces, (size, size))
@@ -170,7 +200,7 @@
     place = lax.shift_right_arithmetic(pieces, 4) * capacity + rank
     slots_ref[...] = jnp.broadcast_to(place, slots_ref.shape)
     lane = lax.broadcasted_iota(I32, (1, size), 1)
-    kept = lane < jnp.minimum(live_ref[0] * PIECES, count)
+    kept = lane < jnp.minimum(live_ref[0, 0] * PIECES, count)
     within = jnp.where(kept, (pieces & (OWNED - 1)) + 1, 0).astype(F32)
     block = tile * capacity
     target = jnp.zeros((block, breadth), F32)
@@ -216,31 +246,31 @@
 
 
 def route_kernel(sizes, *rest):
-    slab, planes, run, breadth = sizes
-    ins, outs = rest[:slab], rest[slab : 2 * slab]
-    tags, tag_sem, sem = rest[2 * slab :]
+    slab, first, last, planes, run, breadth = sizes
+    ins, outs = rest[: last - first], rest[-slab - 2 : -2]
+    tags, tag_sem = rest[-2:]
     here = lax.axis_index("slab")
     reads = [
-        pltpu.make_async_copy(ins[k].at[pl.ds(planes * run, TILE)], tags.at[k], tag_sem.at[k])
-        for k in range(slab)
+        pltpu.make_async_copy(ref.at[pl.ds(planes * run, TILE)], tags.at[k], tag_sem.at[k])
+        for k, ref in enumerate(ins)
     ]
     for read in reads:
         read.start()
-    for k in range(slab):
-        reads[k].wait()
-        for s in range(planes):
+    for read in reads:
+        read.wait()
+    for k, ref in enumerate(ins):
+
+        def move(s, _, k=k, ref=ref):
             target = tags[k, s, breadth - 1].astype(I32)
             rows = pl.ds(pl.multiple_of((target % planes) * run, run), run)
 
-            def act(m, k=k, s=s, rows=rows):
-                source = ins[k].at[pl.ds(s * run, run)]
-                pltpu.make_async_copy(source, outs[m].at[rows], sem.at[k, s]).start()
+            def act(m):
+                outs[m][rows, :] = ref[pl.ds(pl.multiple_of(s * run, run), run), :]
 
             choose((target // planes) ^ here, 0, slab, act)
-    for k in range(slab):
-        for s in range(planes):
-            source = ins[k].at[pl.ds(s * run, run)]
-            pltpu.make_async_copy(source, outs[0].at[pl.ds(0, run)], sem.at[k, s]).wait()
+            return 0
+
+        lax.fori_loop(0, planes, move, 0)
 
 
 def label_kernel(sizes, *rest):
@@ -260,12 +290,15 @@
 
 def spectrum_kernel(live_ref, plane_ref, *rest):
     tabs, out_ref = rest[:6], rest[6]
-
-    def body(t, _):
-        out_ref[t] = forward(plane_ref[t], tabs[0:2], tabs[2:4], tabs[4:6])
+    group = group_of(plane_ref.shape[0])
+
+    def body(i, _):
+        xs = [plane_ref[i * group + n] for n in range(group)]
+        for n, y in enumerate(forward(xs, tabs[0:2], tabs[2:4], tabs[4:6])):
+            out_ref[i * group + n] = y
         return 0
 
-    lax.fori_loop(0, live_ref[0], body, 0)
+    lax.fori_loop(0, (live_ref[0] + group - 1) // group, body, 0)
 
 
 def second_kernel(sizes, live_ref, shift_ref, plane_ref, fixed_ref, *rest):
@@ -304,75 +337,106 @@
     for t in range(held.shape[0]):
         pltpu.make_async_copy(ins[0].at[pl.ds(0, height)], held.at[t], sem.at[t]).wait()
 
-    def body(t, _):
-        partner = held[t]
-        moving = forward(partner, tabs[0:2], tabs[2:4], tabs[4:6])
-        peak = peak_of(fixed_ref[t], moving, tabs[4:6], tabs[6:8], tabs[8:10])
-        weight = weight_of(peak)
-        moved = rolled(partner, shift_ref[1, 0, t], shift_ref[1, 1, t])
-        sum_ref[t] = plane_ref[t] + weight * moved
-        stat_ref[t] = jnp.where(line == 0, jnp.broadcast_to(weight, line.shape), peak)
+    group = group_of(held.shape[0])
+
+    def body(i, _):
+        ts = [i * group + n for n in range(group)]
+        partners = [held[t] for t in ts]
+        moving = forward(partners, tabs[0:2], tabs[2:4], tabs[4:6])
+        fixed = [fixed_ref[t] for t in ts]
+        peaks = peaks_of(fixed, moving, tabs[4:6], tabs[6:8], tabs[8:10])
+        for t, peak in zip(ts, peaks):
+
+            @pl.when(t < live_ref[0])
+            def _(t=t, peak=peak):
+                weight = weight_of(peak)
+                moved = rolled(held[t], shift_ref[1, 0, t], shift_ref[1, 1, t])
+                sum_ref[t] = plane_ref[t] + weight * moved
+                stat_ref[t] = jnp.where(line == 0, jnp.broadcast_to(weight, line.shape), peak)
+
         return 0
 
-    lax.fori_loop(0, live_ref[0], body, 0)
-
-
-def first_kernel(slab, live_ref, shift_ref, slot_ref, sum_ref, stat_ref, fixed_ref, *rest):
+    lax.fori_loop(0, (live_ref[0] + group - 1) // group, body, 0)
+
+
+def first_kernel(slab, live_ref, shift_hbm, slot_vmem, sum_ref, stat_ref, fixed_ref, *rest):
     tabs, ins = rest[:10], rest[10 : 10 + slab]
-    send_ref, peak_ref, plane = rest[10 + slab :]
-    height, breadth = plane.shape
+    send_ref, peak_ref, plane, shift_ref, slot_ref, sem = rest[10 + slab :]
+    group, height, breadth = plane.shape
     run = height // slab
     band = height // PIECES
     here = lax.axis_index("slab")
     line = rows_of((TILE, breadth))
+    small = [
+        pltpu.make_async_copy(shift_hbm, shift_ref, sem.at[0]),
+        pltpu.make_async_copy(slot_vmem, slot_ref, sem.at[1]),
+    ]
+    for copy in small:
+        copy.start()
     peak_ref[...] = jnp.zeros_like(peak_ref)
 
-    def body(t, _):
-        for k in range(slab):
-            rows = pl.ds(pl.multiple_of((here ^ k) * run, run), run)
-            plane[rows, :] = ins[k][pl.ds(pl.multiple_of(t * run, run), run), :]
-        partner = plane[...]
-        moving = forward(partner, tabs[0:2], tabs[2:4], tabs[4:6])
-        peak = peak_of(fixed_ref[t], moving, tabs[4:6], tabs[6:8], tabs[8:10])
-        weight = weight_of(peak)
-        other = stat_ref[t][0:1, 0:1]
-        moved = rolled(partner, shift_ref[0, 0, t], shift_ref[0, 1, t])
-        merged = (sum_ref[t] + weight * moved) / (1.0 + weight + other)
-        peak_ref[t] = jnp.where(line == 0, jnp.broadcast_to(peak, line.shape), stat_ref[t])
-        for b in range(PIECES):
-            start = pl.multiple_of(slot_ref[0, t * PIECES + b] * band, band)
-            send_ref[pl.ds(start, band), :] = merged[b * band : (b + 1) * band]
+    def body(i, _):
+        ts = [i * group + n for n in range(group)]
+        for n, t in enumerate(ts):
+            for k in range(slab):
+                rows = pl.ds(pl.multiple_of((here ^ k) * run, run), run)
+                plane[n, rows, :] = ins[k][pl.ds(pl.multiple_of(t * run, run), run), :]
+        moving = forward([plane[n] for n in range(group)], tabs[0:2], tabs[2:4], tabs[4:6])
+        fixed = [fixed_ref[t] for t in ts]
+        peaks = peaks_of(fixed, moving, tabs[4:6], tabs[6:8], tabs[8:10])
+
+        @pl.when(i == 0)
+        def _():
+            for copy in small:
+                copy.wait()
+
+        for n, t in enumerate(ts):
+
+            @pl.when(t < live_ref[0])
+            def _(n=n, t=t):
+                weight = weight_of(peaks[n])
+                other = stat_ref[t][0:1, 0:1]
+                moved = rolled(plane[n], shift_ref[0, 0, t], shift_ref[0, 1, t])
+                merged = (sum_ref[t] + weight * moved) / (1.0 + weight + other)
+                top = jnp.broadcast_to(peaks[n], line.shape)
+                peak_ref[t] = jnp.where(line == 0, top, stat_ref[t])
+                for b in range(PIECES):
+                    start = pl.multiple_of(slot_ref[0, t * PIECES + b] * band, band)
+                    send_ref[pl.ds(start, band), :] = merged[b * band : (b + 1) * band]
+
         return 0
 
-    lax.fori_loop(0, live_ref[0], body, 0)
+    lax.fori_loop(0, (live_ref[0] + group - 1) // group, body, 0)
 
 
 def gather_kernel(sizes, data_ref, *rest):
     slab, tile, capacity = sizes
     ins, out_ref = rest[:tile], rest[tile]
-    tags, tag_sem = rest[tile + 1 :]
+    total, tags, tag_sem = rest[tile + 1 :]
     band = out_ref.shape[1]
     tile_here = lax.axis_index("tile")
     reads = [pltpu.make_async_copy(ins[m], tags.at[m], tag_sem.at[m]) for m in range(tile)]
     for read in reads:
         read.start()
-    out_ref[...] = jnp.zeros_like(out_ref)
+    total[...] = jnp.zeros_like(total)
     for read in reads:
         read.wait()
 
-    def add(n, _):
-        p, q = n // tile, n % tile
-        for r in range(capacity):
-            label = tags[q ^ tile_here, p, r * TILE].astype(I32)
-            start = pl.multiple_of((n * capacity + r) * band, band)
-
-            @pl.when(label >= 0)
-            def _(label=label, start=start):
-                out_ref[label] += data_ref[pl.ds(start, band), :]
-
+    def add(p, _):
+        for q in range(tile):
+            for r in range(capacity):
+                label = tags[tile_here ^ q, p, r * TILE].astype(I32)
+                target = jnp.where(label < 0, OWNED, label)
+                start = pl.multiple_of(((p * tile + q) * capacity + r) * band, band)
+                total[target] += data_ref[pl.ds(start, band), :]
         return 0
 
-    lax.fori_loop(0, slab * tile, add, 0)
+    lax.fori_loop(0, slab, add, 0)
+    out_ref[...] = total[:OWNED]
+
+
+def group_of(planes):
+    return 2 if planes % 2 == 0 else 1
 
 
 def call(kernel, out_shape, room=4, cost=(1_000_000, 4_000_000), **kwargs):
@@ -411,16 +475,27 @@
         pltpu.with_memory_space_constraint(x, pltpu.HBM)
         for x in (moving_planes, pair_dest, pair_slot, plane_shift)
     ]
+    pieces = pltpu.with_memory_space_constraint(piece_block.reshape(1, count), pltpu.HBM)
+    live_far = live_count.reshape(1, 1)
 
     spread = call(
         functools.partial(spread_kernel, count, (slab, tile, capacity)),
-        [shape((planes * run + block, breadth), F32)] * slab + [shape((TILE, count), I32)],
-        in_specs=[VMEM, SMEM, SMEM, SMEM, HBM],
-        out_specs=[VMEM] * (slab + 1),
-        scratch_shapes=[pltpu.VMEM((slab, block, breadth), F32), dma((slab, planes))],
+        [shape((planes * run + block, breadth), F32)] * slab
+        + [shape((TILE, count), I32), shape((1,), I32)],
+        in_specs=[HBM] * 3 + [pl.BlockSpec(memory_space=pl.ANY), HBM],
+        out_specs=[VMEM] * (slab + 1) + [SMEM],
+        scratch_shapes=[
+            pltpu.VMEM((1, count), I32),
+            pltpu.SMEM(pair_dest.shape, I32),
+            pltpu.SMEM(pair_slot.shape, I32),
+            pltpu.SMEM((1, 1), I32),
+            pltpu.VMEM((slab, block, breadth), F32),
+            dma((4,)),
+            dma((slab,)),
+        ],
         name="spread",
-    )(piece_block.reshape(1, count), pair_dest, pair_slot, live_count, moving_planes)
-    slots = spread[slab]
+    )(pieces, pair_dest, pair_slot, live_far, moving_planes)
+    slots, live_count = spread[slab:]
     runs = exchange(spread[:slab], "slab")
 
     paired = call(
@@ -442,14 +517,17 @@
         name="spectrum",
     )(live_count, fixed_planes, *tabs[:6])
 
-    routed = call(
-        functools.partial(route_kernel, (slab, planes, run, breadth)),
-        [shape((planes * run, breadth), F32)] * slab,
-        in_specs=[VMEM] * slab,
-        out_specs=[VMEM] * slab,
-        scratch_shapes=[pltpu.SMEM((slab, TILE, breadth), F32), dma((slab,)), dma((slab, planes))],
-        name="route",
-    )(*runs)
+    routed = []
+    for name, first, last in (("near", 0, slab // 2), ("far", slab // 2, slab)):
+        routed = call(
+            functools.partial(route_kernel, (slab, first, last, planes, run, breadth)),
+            [shape((planes * run, breadth), F32)] * slab,
+            in_specs=[VMEM] * (last - first + len(routed)),
+            out_specs=[VMEM] * slab,
+            scratch_shapes=[pltpu.SMEM((last - first, TILE, breadth), F32), dma((last - first,))],
+            input_output_aliases={last - first + k: k for k in range(len(routed))},
+            name=name,
+        )(*runs[first:last], *routed)
     first_partners = exchange(routed, "slab")
 
     labels = call(
@@ -481,9 +559,14 @@
     send, tops = call(
         functools.partial(first_kernel, slab),
         [shape((devices * capacity * band, breadth), F32), shape((planes, TILE, breadth), F32)],
-        in_specs=[SMEM, SMEM, SMEM] + [VMEM] * (13 + slab),
+        in_specs=[SMEM, HBM] + [VMEM] * (14 + slab),
         out_specs=[VMEM, VMEM],
-        scratch_shapes=[pltpu.VMEM((height, breadth), F32)],
+        scratch_shapes=[
+            pltpu.VMEM((group_of(planes), height, breadth), F32),
+            pltpu.SMEM(plane_shift.shape, I32),
+            pltpu.SMEM((TILE, count), I32),
+            dma((2,)),
+        ],
         cost=(2 * 10**9, 6 * 10**6),
         room=8,
         name="first",
@@ -497,7 +580,11 @@
         shape((OWNED, band, breadth), F32),
         in_specs=[VMEM] * (tile + 1),
         out_specs=VMEM,
-        scratch_shapes=[pltpu.SMEM((tile, slab, breadth), F32), dma((tile,))],
+        scratch_shapes=[
+            pltpu.VMEM((OWNED + 1, band, breadth), F32),
+            pltpu.SMEM((tile, slab, breadth), F32),
+            dma((tile,)),
+        ],
         room=8,
         name="gather",
     )(arrived.reshape(devices * capacity * band, breadth), *band_labels)

time: 117 us -> 109 us (0.932)
  starting transfers between devices: 47 us -> 42.1 us
  Pallas kernels: 20.4 us -> 18.3 us
    ppermute x20, starting transfers between devices: 35.9 us -> 33.2 us  [exchange(): got[k] = lax.ppermute(arrays[k], axis, [(i, i ^ k) for i in range(size)])]
    all_to_all x1, starting transfers between devices: 11.1 us -> 8.92 us  [local(): lax.all_to_all(send.reshape(devices, capacity * band, breadth), ('slab',...]
    pallas_call x1 -> x2, Pallas kernels: 3.51 us -> 3.02 us  [local(): call(functools.partial(route_kernel, (slab, first, last, planes, run, bre...]
  transfers between devices with their start and end apart: 21 -> 21, of which waited for: 10 -> 9; matrix products, arithmetic and copies ran while one was open for 1% -> 1% of each run, Pallas kernels for 9% -> 10%
where the time goes in v1:
time: 109 us
  waiting for transfers between devices  46.6 us (43%)
  starting transfers between devices  42.1 us (39%)
  Pallas kernels  18.3 us (17%)
  between operations  1.49 us (1%)
    ppermute x20, starting transfers between devices, exchange(): got[k] = lax.ppermute(arrays[k], axis, [(i, i ^ k) for i in range(size)])  33.2 us
    ppermute x20, waiting for transfers between devices, exchange(): got[k] = lax.ppermute(arrays[k], axis, [(i, i ^ k) for i in range(size)])  25.5 us
    all_to_all x1, waiting for transfers between devices, local(): lax.all_to_all(send.reshape(devices, capacity * band, breadth), ('slab',...  21.1 us
    all_to_all x1, starting transfers between devices, local(): lax.all_to_all(send.reshape(devices, capacity * band, breadth), ('slab',...  8.92 us
    pallas_call x1, Pallas kernels, local(): call(functools.partial(second_kernel, (tile, tile_capacity)), [shape((pla...  4.33 us
    pallas_call x1, Pallas kernels, local(): call(functools.partial(first_kernel, slab), [shape((devices * capacity *...  3.65 us
    pallas_call x2, Pallas kernels, local(): call(functools.partial(route_kernel, (slab, first, last, planes, run, bre...  3.02 us
  transfers between devices with their start and end apart: 21, of which 9 were waited for; matrix products, arithmetic and copies ran while one was open for 1% of the time, Pallas kernels for 10%

profile of v1, /device:TPU:0, one launch (start us, length us, event | category | flops | bytes accessed | tf_op | source)
XLA Modules:
  0.0 109.2 jit_solution(3987242411550456396)
XLA Ops:
  1.3 1.9 %spread.1 = (f32[264,128]{1,0:T(8,128)S(1)}, f32[264,128]{1,0:T(8,128)S(1)}, f32[264,128]{1,0:T(8,128)S(1)}, f32[264,128]{1,0:T(8,128)S(1)}, f32[264,128]{1,0:T(...) custom-call(s32[1,64]{1,0:T(1,128)} %bitcast.10, ...), custom_call_target="tpu_custom_call" | custom-call | flops 1000000 | bytes 4000000 | tf_op jit(solution)/shard_map/spread/pallas_call | solution.py:481
  3.2 4.1 %collective-permute-start.3 = (f32[264,128]{1,0:T(8,128)S(1)}, f32[264,128]{1,0:T(8,128)S(1)}, u32[]{:S(2)}, u32[]{:S(2)}) collective-permute-start(f32[264,128]{1,0:T(8,128)S(1)} %get-tuple-element.46), channel_id=1, source_target_pairs={{0,16},{4,20},{8,24},{12,28},{16,0},{20,4},{24,8},{28,12},{1,17},{... | collective-permute-start | bytes 405512 | tf_op jit(solution)/shard_map/ppermute | solution.py:456
  8.9 2.1 %pair.1 = (f32[1032,128]{1,0:T(8,128)S(1)}, f32[1032,128]{1,0:T(8,128)S(1)}, f32[1032,128]{1,0:T(8,128)S(1)}, f32[1032,128]{1,0:T(8,128)S(1)}) custom-call(s32[2,4]{1,0:T(2,128)} %dest_ref.1, s32[2,4]{1,0:T(2,128)} %slot_ref.1, f32[2,4,512,128]{3,2,1,0:T(8,128)} %moving_ref.3, s32[8,64]{1,0:T(8,128)S(1)} %get-tuple-element.41.after_ref.slot_vmem), custom_call_target="tpu_custom_call" | custom-call | flops 1000000 | bytes 4000000 | tf_op jit(solution)/shard_map/pair/pallas_call | solution.py:501
  11.1 1.8 %collective-permute-start.1 = (f32[1032,128]{1,0:T(8,128)S(1)}, f32[1032,128]{1,0:T(8,128)S(1)}, u32[]{:S(2)}, u32[]{:S(2)}) collective-permute-start(f32[1032,128]{1,0:T(8,128)S(1)} %get-tuple-element.44), channel_id=1, source_target_pairs={{0,2},{1,3},{2,0},{3,1},{4,6},{5,7},{6,4},{7,5},{8,10},{9,11},{10,... | collective-permute-start | bytes 1585160 | tf_op jit(solution)/shard_map/ppermute | solution.py:456
  12.9 4.6 %collective-permute-done.3.rest_0_.rest_4_ = f32[264,128]{1,0:T(8,128)S(1)} collective-permute-done((f32[264,128]{1,0:T(8,128)S(1)}, f32[264,128]{1,0:T(8,128)S(1)}, u32[]{:S(2)}, u32[]{:S(2)}) %collective-permute-start.3) | collective-permute-done | bytes 135200 | tf_op jit(solution)/shard_map/ppermute | solution.py:456
  17.6 3.0 %collective-permute-done.4.rest_1_.rest_5_ = f32[264,128]{1,0:T(8,128)S(1)} collective-permute-done((f32[264,128]{1,0:T(8,128)S(1)}, f32[264,128]{1,0:T(8,128)S(1)}, u32[]{:S(2)}, u32[]{:S(2)}) %collective-permute-start.4) | collective-permute-done | bytes 135200 | tf_op jit(solution)/shard_map/ppermute | solution.py:456
  20.6 1.9 %collective-permute-start.9 = (f32[264,128]{1,0:T(8,128)S(1)}, f32[264,128]{1,0:T(8,128)S(1)}, u32[]{:S(2)}, u32[]{:S(2)}) collective-permute-start(f32[264,128]{1,0:T(8,128)S(1)} %get-tuple-element.53), channel_id=1, source_target_pairs={{0,12},{4,8},{8,4},{12,0},{16,28},{20,24},{24,20},{28,16},{1,13},{... | collective-permute-start | bytes 405512 | tf_op jit(solution)/shard_map/ppermute | solution.py:456
  22.5 4.0 %collective-permute-done.8.rest_2_ = f32[264,128]{1,0:T(8,128)S(1)} collective-permute-done((f32[264,128]{1,0:T(8,128)S(1)}, f32[264,128]{1,0:T(8,128)S(1)}, u32[]{:S(2)}, u32[]{:S(2)}) %collective-permute-start.8) | collective-permute-done | bytes 135200 | tf_op jit(solution)/shard_map/ppermute | solution.py:456
  26.5 4.0 %collective-permute-start.5 = (f32[264,128]{1,0:T(8,128)S(1)}, f32[264,128]{1,0:T(8,128)S(1)}, u32[]{:S(2)}, u32[]{:S(2)}) collective-permute-start(f32[264,128]{1,0:T(8,128)S(1)} %get-tuple-element.48), channel_id=1, source_target_pairs={{0,24},{4,28},{8,16},{12,20},{16,8},{20,12},{24,0},{28,4},{1,25},{... | collective-permute-start | bytes 405512 | tf_op jit(solution)/shard_map/ppermute | solution.py:456
  30.5 2.8 %collective-permute-start.6 = (f32[264,128]{1,0:T(8,128)S(1)}, f32[264,128]{1,0:T(8,128)S(1)}, u32[]{:S(2)}, u32[]{:S(2)}) collective-permute-start(f32[264,128]{1,0:T(8,128)S(1)} %get-tuple-element.49), channel_id=1, source_target_pairs={{0,28},{4,24},{8,20},{12,16},{16,12},{20,8},{24,4},{28,0},{1,29},{... | collective-permute-start | bytes 405512 | tf_op jit(solution)/shard_map/ppermute | solution.py:456
  34.9 3.4 %collective-permute-done.6.rest_3_.rest_7_ = f32[264,128]{1,0:T(8,128)S(1)} collective-permute-done((f32[264,128]{1,0:T(8,128)S(1)}, f32[264,128]{1,0:T(8,128)S(1)}, u32[]{:S(2)}, u32[]{:S(2)}) %collective-permute-start.6) | collective-permute-done | bytes 135200 | tf_op jit(solution)/shard_map/ppermute | solution.py:456
  40.5 3.6 %collective-permute-start.11 = (f32[256,128]{1,0:T(8,128)S(1)}, f32[256,128]{1,0:T(8,128)S(1)}, u32[]{:S(2)}, u32[]{:S(2)}) collective-permute-start(f32[256,128]{1,0:T(8,128)S(1)} %get-tuple-element.66), channel_id=1, source_target_pairs={{0,8},{4,12},{8,0},{12,4},{16,24},{20,28},{24,16},{28,20},{1,9},{5... | collective-permute-start | bytes 393224 | tf_op jit(solution)/shard_map/ppermute | solution.py:456
  45.6 3.0 %collective-permute-start.12 = (f32[256,128]{1,0:T(8,128)S(1)}, f32[256,128]{1,0:T(8,128)S(1)}, u32[]{:S(2)}, u32[]{:S(2)}) collective-permute-start(f32[256,128]{1,0:T(8,128)S(1)} %get-tuple-element.67), channel_id=1, source_target_pairs={{0,12},{4,8},{8,4},{12,0},{16,28},{20,24},{24,20},{28,16},{1,13},{... | collective-permute-start | bytes 393224 | tf_op jit(solution)/shard_map/ppermute | solution.py:456
  48.6 1.9 %collective-permute-start.13 = (f32[256,128]{1,0:T(8,128)S(1)}, f32[256,128]{1,0:T(8,128)S(1)}, u32[]{:S(2)}, u32[]{:S(2)}) collective-permute-start(f32[256,128]{1,0:T(8,128)S(1)} %get-tuple-element.68), channel_id=1, source_target_pairs={{0,16},{4,20},{8,24},{12,28},{16,0},{20,4},{24,8},{28,12},{1,17},{... | collective-permute-start | bytes 393224 | tf_op jit(solution)/shard_map/ppermute | solution.py:456
  51.5 2.8 %collective-permute-start.15 = (f32[256,128]{1,0:T(8,128)S(1)}, f32[256,128]{1,0:T(8,128)S(1)}, u32[]{:S(2)}, u32[]{:S(2)}) collective-permute-start(f32[256,128]{1,0:T(8,128)S(1)} %get-tuple-element.70), channel_id=1, source_target_pairs={{0,24},{4,28},{8,16},{12,20},{16,8},{20,12},{24,0},{28,4},{1,25},{... | collective-permute-start | bytes 393224 | tf_op jit(solution)/shard_map/ppermute | solution.py:456
  54.3 2.0 %collective-permute-start.16 = (f32[256,128]{1,0:T(8,128)S(1)}, f32[256,128]{1,0:T(8,128)S(1)}, u32[]{:S(2)}, u32[]{:S(2)}) collective-permute-start(f32[256,128]{1,0:T(8,128)S(1)} %get-tuple-element.71), channel_id=1, source_target_pairs={{0,28},{4,24},{8,20},{12,16},{16,12},{20,8},{24,4},{28,0},{1,29},{... | collective-permute-start | bytes 393224 | tf_op jit(solution)/shard_map/ppermute | solution.py:456
  56.2 4.3 %second.1 = (f32[4,512,128]{2,1,0:T(8,128)S(1)}, f32[4,8,128]{2,1,0:T(8,128)S(1)}) custom-call(s32[1]{0:T(128)} %get-tuple-element.40.live_ref, s32[2,2,4]{2,1,0:T(2,128)} %shift_hbm.1, f32[4,512,128]{2,1,0:T(8,128)S(1)} %copy-done, f32[4,272,256]{2,1,0:T(8,128)S(1)} %spectrum.1.fixed_ref, bf16[256,256]{1,0:T(8,128)(2,1)S(1)} %copy-done.6, ...), custom_call_target="tpu_custom_call" | custom-call | flops 2000000000 | bytes 6000000 | tf_op jit(solution)/shard_map/second/pallas_call | solution.py:542
  60.6 4.9 %collective-permute-done.13.rest_14_ = f32[256,128]{1,0:T(8,128)S(1)} collective-permute-done((f32[256,128]{1,0:T(8,128)S(1)}, f32[256,128]{1,0:T(8,128)S(1)}, u32[]{:S(2)}, u32[]{:S(2)}) %collective-permute-start.13) | collective-permute-done | bytes 131104 | tf_op jit(solution)/shard_map/ppermute | solution.py:456
  65.5 3.0 %collective-permute-done.14.rest_15_ = f32[256,128]{1,0:T(8,128)S(1)} collective-permute-done((f32[256,128]{1,0:T(8,128)S(1)}, f32[256,128]{1,0:T(8,128)S(1)}, u32[]{:S(2)}, u32[]{:S(2)}) %collective-permute-start.14) | collective-permute-done | bytes 131104 | tf_op jit(solution)/shard_map/ppermute | solution.py:456
  68.5 3.7 %first.1 = (f32[2048,128]{1,0:T(8,128)}, f32[4,8,128]{2,1,0:T(8,128)S(1)}) custom-call(s32[1]{0:T(128)} %get-tuple-element.40.live_ref, s32[2,2,4]{2,1,0:T(2,128)} %shift_hbm.1, s32[8,64]{1,0:T(8,128)S(1)} %get-tuple-element.41.after_ref.slot_vmem, f32[4,512,128]{2,1,0:T(8,128)S(1)} %get-tuple-element.63.sum_ref, ...), custom_call_target="tpu_custom_call" | custom-call | flops 2000000000 | bytes 6000000 | tf_op jit(solution)/shard_map/first/pallas_call | solution.py:559
  72.1 8.9 %all-to-all-start = ((f32[32,64,128]{2,1,0:T(8,128)}), f32[32,64,128]{2,1,0:T(8,128)S(1)}, u32[]{:S(2)}, u32[]{:S(2)}) async-start(f32[32,64,128]{2,1,0:T(8,128)} %bitcast.4), calls=%async_computation | async-start | bytes 2097152 | tf_op jit(solution)/shard_map/all_to_all | solution.py:575
  83.7 2.1 %collective-permute-done.18.rest_2_ = f32[8,128]{1,0:T(8,128)S(1)} collective-permute-done((f32[8,128]{1,0:T(8,128)S(1)}, f32[8,128]{1,0:T(8,128)S(1)}, u32[]{:S(2)}, u32[]{:S(2)}) %collective-permute-start.18) | collective-permute-done | bytes 4128 | tf_op jit(solution)/shard_map/ppermute | solution.py:456
  86.2 21.1 %all-to-all-done = f32[32,64,128]{2,1,0:T(8,128)S(1)} async-done(((f32[32,64,128]{2,1,0:T(8,128)}), f32[32,64,128]{2,1,0:T(8,128)S(1)}, u32[]{:S(2)}, u32[]{:S(2)}) %all-to-all-start) | async-done | bytes 1048608 | tf_op jit(solution)/shard_map/all_to_all | solution.py:575
  107.3 1.9 %gather.1 = f32[16,32,128]{2,1,0:T(8,128)} custom-call(f32[2048,128]{1,0:T(8,128)S(1)} %bitcast.8, f32[8,128]{1,0:T(8,128)S(1)} %get-tuple-element.74.rest_0_, f32[8,128]{1,0:T(8,128)S(1)} %collective-permute-done.17.rest_1_, f32[8,128]{1,0:T(8,128)S(1)} %collective-permute-done.18.rest_2_, f32[8,128]{1,0:T(8,128)S(1)} %collective-permute-done.19.rest_3_), custom_call_target="tpu_custom_call" | custom-call | flops 1000000 | bytes 4000000 | tf_op jit(solution)/shard_map/gather/pallas_call | solution.py:578
  (51 shorter events, 10.7 us)
Async XLA Ops:
  3.2 14.4 %collective-permute-start.3 = (f32[264,128]{1,0:T(8,128)S(1)}, f32[264,128]{1,0:T(8,128)S(1)}, u32[]{:S(2)}, u32[]{:S(2)}) collective-permute-start(f32[264,128]{1,0:T(8,128)S(1)} %get-tuple-element.46), channel_id=1, source_target_pairs={{0,16},{4,20},{8,24},{12,28},{16,0},{20,4},{24,8},{28,12},{1,17},{... | collective-permute-start | bytes 405512 | tf_op jit(solution)/shard_map/ppermute | solution.py:456
  7.3 13.3 %collective-permute-start.4 = (f32[264,128]{1,0:T(8,128)S(1)}, f32[264,128]{1,0:T(8,128)S(1)}, u32[]{:S(2)}, u32[]{:S(2)}) collective-permute-start(f32[264,128]{1,0:T(8,128)S(1)} %get-tuple-element.47), channel_id=1, source_target_pairs={{0,20},{4,16},{8,28},{12,24},{16,4},{20,0},{24,12},{28,8},{1,21},{... | collective-permute-start | bytes 405512 | tf_op jit(solution)/shard_map/ppermute | solution.py:456
  8.6 12.0 %collective-permute-start.7 = (f32[264,128]{1,0:T(8,128)S(1)}, f32[264,128]{1,0:T(8,128)S(1)}, u32[]{:S(2)}, u32[]{:S(2)}) collective-permute-start(f32[264,128]{1,0:T(8,128)S(1)} %get-tuple-element.51), channel_id=1, source_target_pairs={{0,4},{4,0},{8,12},{12,8},{16,20},{20,16},{24,28},{28,24},{1,5},{5... | collective-permute-start | bytes 405512 | tf_op jit(solution)/shard_map/ppermute | solution.py:456
  8.9 35.3 %copy-start.2 = (bf16[256,256]{1,0:T(8,128)(2,1)S(1)}, bf16[256,256]{1,0:T(8,128)(2,1)}, u32[]{:S(2)}) copy-start(bf16[256,256]{1,0:T(8,128)(2,1)} %constant.24.clone.rest_4_) | copy-start | bytes 393220
  8.9 35.3 %copy-start.3 = (bf16[256,256]{1,0:T(8,128)(2,1)S(1)}, bf16[256,256]{1,0:T(8,128)(2,1)}, u32[]{:S(2)}) copy-start(bf16[256,256]{1,0:T(8,128)(2,1)} %constant.23.clone.rest_3_) | copy-start | bytes 393220
  8.9 35.3 %copy-start.4 = (bf16[256,256]{1,0:T(8,128)(2,1)S(1)}, bf16[256,256]{1,0:T(8,128)(2,1)}, u32[]{:S(2)}) copy-start(bf16[256,256]{1,0:T(8,128)(2,1)} %constant.22.clone.rest_2_) | copy-start | bytes 393220
  11.0 39.4 %collective-permute-start = (f32[1032,128]{1,0:T(8,128)S(1)}, f32[1032,128]{1,0:T(8,128)S(1)}, u32[]{:S(2)}, u32[]{:S(2)}) collective-permute-start(f32[1032,128]{1,0:T(8,128)S(1)} %get-tuple-element.43), channel_id=1, source_target_pairs={{0,1},{1,0},{2,3},{3,2},{4,5},{5,4},{6,7},{7,6},{8,9},{9,8},{10,11... | collective-permute-start | bytes 1585160 | tf_op jit(solution)/shard_map/ppermute | solution.py:456
  11.1 40.4 %collective-permute-start.1 = (f32[1032,128]{1,0:T(8,128)S(1)}, f32[1032,128]{1,0:T(8,128)S(1)}, u32[]{:S(2)}, u32[]{:S(2)}) collective-permute-start(f32[1032,128]{1,0:T(8,128)S(1)} %get-tuple-element.44), channel_id=1, source_target_pairs={{0,2},{1,3},{2,0},{3,1},{4,6},{5,7},{6,4},{7,5},{8,10},{9,11},{10,... | collective-permute-start | bytes 1585160 | tf_op jit(solution)/shard_map/ppermute | solution.py:456
  17.6 36.7 %collective-permute-start.2 = (f32[1032,128]{1,0:T(8,128)S(1)}, f32[1032,128]{1,0:T(8,128)S(1)}, u32[]{:S(2)}, u32[]{:S(2)}) collective-permute-start(f32[1032,128]{1,0:T(8,128)S(1)} %get-tuple-element.45), channel_id=1, source_target_pairs={{0,3},{1,2},{2,1},{3,0},{4,7},{5,6},{6,5},{7,4},{8,11},{9,10},{10,... | collective-permute-start | bytes 1585160 | tf_op jit(solution)/shard_map/ppermute | solution.py:456
  20.6 5.9 %collective-permute-start.8 = (f32[264,128]{1,0:T(8,128)S(1)}, f32[264,128]{1,0:T(8,128)S(1)}, u32[]{:S(2)}, u32[]{:S(2)}) collective-permute-start(f32[264,128]{1,0:T(8,128)S(1)} %get-tuple-element.52), channel_id=1, source_target_pairs={{0,8},{4,12},{8,0},{12,4},{16,24},{20,28},{24,16},{28,20},{1,9},{5... | collective-permute-start | bytes 405512 | tf_op jit(solution)/shard_map/ppermute | solution.py:456
  20.6 9.9 %collective-permute-start.9 = (f32[264,128]{1,0:T(8,128)S(1)}, f32[264,128]{1,0:T(8,128)S(1)}, u32[]{:S(2)}, u32[]{:S(2)}) collective-permute-start(f32[264,128]{1,0:T(8,128)S(1)} %get-tuple-element.53), channel_id=1, source_target_pairs={{0,12},{4,8},{8,4},{12,0},{16,28},{20,24},{24,20},{28,16},{1,13},{... | collective-permute-start | bytes 405512 | tf_op jit(solution)/shard_map/ppermute | solution.py:456
  26.5 8.4 %collective-permute-start.5 = (f32[264,128]{1,0:T(8,128)S(1)}, f32[264,128]{1,0:T(8,128)S(1)}, u32[]{:S(2)}, u32[]{:S(2)}) collective-permute-start(f32[264,128]{1,0:T(8,128)S(1)} %get-tuple-element.48), channel_id=1, source_target_pairs={{0,24},{4,28},{8,16},{12,20},{16,8},{20,12},{24,0},{28,4},{1,25},{... | collective-permute-start | bytes 405512 | tf_op jit(solution)/shard_map/ppermute | solution.py:456
  30.5 7.8 %collective-permute-start.6 = (f32[264,128]{1,0:T(8,128)S(1)}, f32[264,128]{1,0:T(8,128)S(1)}, u32[]{:S(2)}, u32[]{:S(2)}) collective-permute-start(f32[264,128]{1,0:T(8,128)S(1)} %get-tuple-element.49), channel_id=1, source_target_pairs={{0,28},{4,24},{8,20},{12,16},{16,12},{20,8},{24,4},{28,0},{1,29},{... | collective-permute-start | bytes 405512 | tf_op jit(solution)/shard_map/ppermute | solution.py:456
  39.9 5.6 %collective-permute-start.10 = (f32[256,128]{1,0:T(8,128)S(1)}, f32[256,128]{1,0:T(8,128)S(1)}, u32[]{:S(2)}, u32[]{:S(2)}) collective-permute-start(f32[256,128]{1,0:T(8,128)S(1)} %get-tuple-element.65), channel_id=1, source_target_pairs={{0,4},{4,0},{8,12},{12,8},{16,20},{20,16},{24,28},{28,24},{1,5},{5... | collective-permute-start | bytes 393224 | tf_op jit(solution)/shard_map/ppermute | solution.py:456
  40.5 8.0 %collective-permute-start.11 = (f32[256,128]{1,0:T(8,128)S(1)}, f32[256,128]{1,0:T(8,128)S(1)}, u32[]{:S(2)}, u32[]{:S(2)}) collective-permute-start(f32[256,128]{1,0:T(8,128)S(1)} %get-tuple-element.66), channel_id=1, source_target_pairs={{0,8},{4,12},{8,0},{12,4},{16,24},{20,28},{24,16},{28,20},{1,9},{5... | collective-permute-start | bytes 393224 | tf_op jit(solution)/shard_map/ppermute | solution.py:456
  45.6 15.0 %collective-permute-start.12 = (f32[256,128]{1,0:T(8,128)S(1)}, f32[256,128]{1,0:T(8,128)S(1)}, u32[]{:S(2)}, u32[]{:S(2)}) collective-permute-start(f32[256,128]{1,0:T(8,128)S(1)} %get-tuple-element.67), channel_id=1, source_target_pairs={{0,12},{4,8},{8,4},{12,0},{16,28},{20,24},{24,20},{28,16},{1,13},{... | collective-permute-start | bytes 393224 | tf_op jit(solution)/shard_map/ppermute | solution.py:456
  48.6 17.0 %collective-permute-start.13 = (f32[256,128]{1,0:T(8,128)S(1)}, f32[256,128]{1,0:T(8,128)S(1)}, u32[]{:S(2)}, u32[]{:S(2)}) collective-permute-start(f32[256,128]{1,0:T(8,128)S(1)} %get-tuple-element.68), channel_id=1, source_target_pairs={{0,16},{4,20},{8,24},{12,28},{16,0},{20,4},{24,8},{28,12},{1,17},{... | collective-permute-start | bytes 393224 | tf_op jit(solution)/shard_map/ppermute | solution.py:456
  50.5 18.0 %collective-permute-start.14 = (f32[256,128]{1,0:T(8,128)S(1)}, f32[256,128]{1,0:T(8,128)S(1)}, u32[]{:S(2)}, u32[]{:S(2)}) collective-permute-start(f32[256,128]{1,0:T(8,128)S(1)} %get-tuple-element.69), channel_id=1, source_target_pairs={{0,20},{4,16},{8,28},{12,24},{16,4},{20,0},{24,12},{28,8},{1,21},{... | collective-permute-start | bytes 393224 | tf_op jit(solution)/shard_map/ppermute | solution.py:456
  51.5 17.0 %collective-permute-start.15 = (f32[256,128]{1,0:T(8,128)S(1)}, f32[256,128]{1,0:T(8,128)S(1)}, u32[]{:S(2)}, u32[]{:S(2)}) collective-permute-start(f32[256,128]{1,0:T(8,128)S(1)} %get-tuple-element.70), channel_id=1, source_target_pairs={{0,24},{4,28},{8,16},{12,20},{16,8},{20,12},{24,0},{28,4},{1,25},{... | collective-permute-start | bytes 393224 | tf_op jit(solution)/shard_map/ppermute | solution.py:456
  54.3 14.2 %collective-permute-start.16 = (f32[256,128]{1,0:T(8,128)S(1)}, f32[256,128]{1,0:T(8,128)S(1)}, u32[]{:S(2)}, u32[]{:S(2)}) collective-permute-start(f32[256,128]{1,0:T(8,128)S(1)} %get-tuple-element.71), channel_id=1, source_target_pairs={{0,28},{4,24},{8,20},{12,16},{16,12},{20,8},{24,4},{28,0},{1,29},{... | collective-permute-start | bytes 393224 | tf_op jit(solution)/shard_map/ppermute | solution.py:456
  72.1 35.1 %all-to-all-start = ((f32[32,64,128]{2,1,0:T(8,128)}), f32[32,64,128]{2,1,0:T(8,128)S(1)}, u32[]{:S(2)}, u32[]{:S(2)}) async-start(f32[32,64,128]{2,1,0:T(8,128)} %bitcast.4), calls=%async_computation | async-start | bytes 2097152 | tf_op jit(solution)/shard_map/all_to_all | solution.py:575
  81.1 2.6 %collective-permute-start.17 = (f32[8,128]{1,0:T(8,128)S(1)}, f32[8,128]{1,0:T(8,128)S(1)}, u32[]{:S(2)}, u32[]{:S(2)}) collective-permute-start(f32[8,128]{1,0:T(8,128)S(1)} %get-tuple-element.75), channel_id=1, source_target_pairs={{0,1},{1,0},{2,3},{3,2},{4,5},{5,4},{6,7},{7,6},{8,9},{9,8},{10,11... | collective-permute-start | bytes 12296 | tf_op jit(solution)/shard_map/ppermute | solution.py:456
  81.4 4.4 %collective-permute-start.18 = (f32[8,128]{1,0:T(8,128)S(1)}, f32[8,128]{1,0:T(8,128)S(1)}, u32[]{:S(2)}, u32[]{:S(2)}) collective-permute-start(f32[8,128]{1,0:T(8,128)S(1)} %get-tuple-element.76), channel_id=1, source_target_pairs={{0,2},{1,3},{2,0},{3,1},{4,6},{5,7},{6,4},{7,5},{8,10},{9,11},{10,... | collective-permute-start | bytes 12296 | tf_op jit(solution)/shard_map/ppermute | solution.py:456
  83.1 3.1 %collective-permute-start.19 = (f32[8,128]{1,0:T(8,128)S(1)}, f32[8,128]{1,0:T(8,128)S(1)}, u32[]{:S(2)}, u32[]{:S(2)}) collective-permute-start(f32[8,128]{1,0:T(8,128)S(1)} %get-tuple-element.77), channel_id=1, source_target_pairs={{0,3},{1,2},{2,1},{3,0},{4,7},{5,6},{6,5},{7,4},{8,11},{9,10},{10,... | collective-permute-start | bytes 12296 | tf_op jit(solution)/shard_map/ppermute | solution.py:456
  (8 other events, 206.4 us)
